TPU v7x, 32 devices: a whole 2x2x4 slice. The times are simulated.
32 devices in a mesh: dp: 8 (over z, y), expert: 4 (over x, core).
Axes of the slice: x: 2, y: 2, z: 4, core: 2. Of those that a mesh axis runs over, the one named last changes fastest.
Arguments:
- patches: float32 [32, 512, 384], P(('dp', 'expert')), may hold values from -6 to 6
- image_ids: int32 [32, 512], P(('dp', 'expert')), may hold values from 0 to 5, never falling along the last dimension, each value on 1 to 196 neighbouring positions
- pad_mask: int32 [32, 512], P(('dp', 'expert')), may hold values 0 or 1
- ln1_gain: float32 [384], replicated, may hold values from 0.5 to 1.5
- ln1_bias: float32 [384], replicated, may hold values from -3 to 3
- w_qkv: float32 [384, 1152], replicated, may hold values from -0.3125 to 0.3125
- bias_qv: float32 [2, 384], replicated, may hold values from -3 to 3
- w_out: float32 [384, 384], replicated, may hold values from -1.25 to 1.25
- bias_out: float32 [384], replicated, may hold values from -3 to 3
- ln2_gain: float32 [384], replicated, may hold values from 0.5 to 1.5
- ln2_bias: float32 [384], replicated, may hold values from -2 to 2
- slot_keys: float32 [384, 8], replicated, may hold values from -0.625 to 0.625
- w_in: float32 [8, 384, 1536], P('expert'), may hold values from -1.25 to 1.25
- bias_in: float32 [8, 1536], P('expert'), may hold values from -3 to 3
- w_down: float32 [8, 1536, 384], P('expert'), may hold values from -0.3125 to 0.3125
- bias_down: float32 [8, 384], P('expert'), may hold values from -3 to 3
- cotangent: float32 [32, 512, 384], P(('dp', 'expert')), may hold values from -6 to 6
Outputs:
- activations: float32 [32, 512, 384], P(('dp', 'expert'))
- grad_patches: float32 [32, 512, 384], P(('dp', 'expert'))
- grad_ln1_gain: float32 [384], replicated
- grad_ln1_bias: float32 [384], replicated
- grad_w_qkv: float32 [384, 1152], replicated
- grad_bias_qv: float32 [2, 384], replicated
- grad_w_out: float32 [384, 384], replicated
- grad_bias_out: float32 [384], replicated
- grad_ln2_gain: float32 [384], replicated
- grad_ln2_bias: float32 [384], replicated
- grad_slot_keys: float32 [384, 8], replicated
- grad_w_in: float32 [8, 384, 1536], P('expert')
- grad_bias_in: float32 [8, 1536], P('expert')
- grad_w_down: float32 [8, 1536, 384], P('expert')
- grad_bias_down: float32 [8, 384], P('expert')
All inputs are finite; a program needn't handle non-finite values. No bound on the sum of `pad_mask` on one device may be relied on, other than what follows from the above.
Results may differ from a plain program's by a relative error of at most 0.0003.
Values sent between devices are 32-bit elements; how exact they have to be, the bound alone decides.
A program may use at most 128 MiB of HBM per device.

v0:
```python
import functools
import math

import jax
import jax.numpy as jnp
from jax import lax
from jax.experimental import pallas as pl
from jax.experimental.pallas import tpu as pltpu
from jax.sharding import PartitionSpec as P

HEADS = 6
HEAD_DIM = 64
LANES = 128
EPSILON = 1e-06
NEGATIVE = -1e30
HIGH = lax.Precision.HIGH
BF = jnp.bfloat16
F32 = jnp.float32
MESH = pl.DeviceIdType.MESH
VMEM = pl.BlockSpec(memory_space=pltpu.VMEM)
ANY = pl.BlockSpec(memory_space=pl.ANY)


def dot(left, right, dim_left, dim_right, precision=HIGH):
    return lax.dot_general(
        left, right, (((dim_left,), (dim_right,)), ((), ())), precision=precision, preferred_element_type=F32
    )


def parts(value):
    high = value.astype(BF)
    return high, (value - high.astype(F32)).astype(BF)


def norm_stats(values):
    center = values - jnp.mean(values, -1, keepdims=True)
    spread = jnp.mean(center * center, -1, keepdims=True)
    scale = lax.rsqrt(spread + EPSILON)
    return center * scale, scale


def column(row):
    return jnp.broadcast_to(row, (8, row.shape[1])).T[:, :1]


def to_tiles(rows):
    return jnp.stack([jnp.concatenate([rows[e : e + 1, LANES * i : LANES * (i + 1)] for i in range(8)], 0) for e in range(rows.shape[0])], 0)


def from_tiles(tiles, first, count):
    return jnp.concatenate([tiles[:, first + i, :] for i in range(count)], -1)


def front_kernel(x_ref, ids_ref, live_ref, g1_ref, b1_ref, wqkv_ref, bqv_ref, wout_ref, bout_ref, g2_ref, b2_ref,
                 keys_ref, cot_ref, resid_ref, joined_ref, context_ref, attn_ref, logits_ref, stats_ref, block_ref):
    x = x_ref[0]
    length, width = x.shape
    hat, _ = norm_stats(x)
    normed = hat * g1_ref[...] + b1_ref[...]
    joined = dot(wqkv_ref[...], normed, 0, 1)
    bias = jnp.broadcast_to(bqv_ref[0:1], (8, width)).T[:, :1]
    bias_v = jnp.broadcast_to(bqv_ref[1:2], (8, width)).T[:, :1]
    scale = 1.0 / math.sqrt(HEAD_DIM)
    joined_ref[0:width] = (joined[:width] + bias) * scale
    joined_ref[width : 2 * width] = joined[width : 2 * width]
    joined_ref[2 * width :] = joined[2 * width :] + bias_v
    ids = ids_ref[...].astype(F32)
    block_ref[...] = jnp.where(column(ids) == ids, 0.0, NEGATIVE)
    half = length // 2
    for h in range(HEADS):
        at = HEAD_DIM * h
        q_hi, q_lo = parts(joined_ref[at : at + HEAD_DIM])
        k_hi, k_lo = parts(joined_ref[width + at : width + at + HEAD_DIM])
        v_hi, v_lo = parts(joined_ref[2 * width + at : 2 * width + at + HEAD_DIM])
        queries = jnp.concatenate([q_hi, q_hi, q_lo], 0)
        keys = jnp.concatenate([k_hi, k_lo, k_hi], 0).T
        values = jnp.concatenate([v_hi, v_lo], 0)
        for b in range(2):
            span = slice(half * b, half * (b + 1))
            scores = dot(keys, queries[:, span], 1, 0, None) + block_ref[:, span]
            expo = jnp.exp(scores - jnp.max(scores, 0, keepdims=True))
            attn = expo * (1.0 / jnp.sum(expo, 0, keepdims=True))
            attn_ref[h, :, span] = attn
            p_hi, p_lo = parts(attn)
            both = dot(values, p_hi, 1, 0, None)
            context_ref[at : at + HEAD_DIM, span] = both[:HEAD_DIM] + both[HEAD_DIM:] + dot(v_hi, p_lo, 1, 0, None)
    resid = x + dot(context_ref[...], wout_ref[...], 0, 0) + bout_ref[...]
    resid_ref[...] = resid
    hat2, _ = norm_stats(resid)
    normed2 = hat2 * g2_ref[...] + b2_ref[...]
    logits = dot(keys_ref[...], normed2, 0, 1)
    logits_ref[...] = logits
    masked = jnp.where(live_ref[...] > 0, logits, NEGATIVE)
    peak = jnp.max(masked, 1, keepdims=True)
    expo = jnp.exp(masked - peak)
    total = jnp.sum(expo, 1, keepdims=True)
    summed = dot(expo, normed2, 1, 0)
    top = jnp.max(logits, 0, keepdims=True)
    comb = jnp.exp(logits - top)
    comb = comb * (1.0 / jnp.sum(comb, 0, keepdims=True))
    part_out = dot(comb, cot_ref[0], 1, 0)
    experts = logits.shape[0]
    rows = jnp.concatenate([summed, part_out, jnp.broadcast_to(peak, (experts, LANES)), jnp.broadcast_to(total, (experts, LANES))], 1)
    stats_ref[...] = to_tiles(rows)


def merge(tiles):
    peaks = [tile[:, 6:7, :] for tile in tiles]
    peak = functools.reduce(jnp.maximum, peaks)
    row = lax.broadcasted_iota(jnp.int32, tiles[0].shape, 1)
    weighted = (row < 3) | (row == 7)
    total = None
    for tile, own in zip(tiles, peaks):
        scaled = jnp.where(weighted, tile * jnp.exp(own - peak), tile)
        total = scaled if total is None else total + scaled
    return jnp.where(row == 6, peak, total)


def gelu_parts(inner):
    phi = 0.5 * (1.0 + lax.erf(inner * (1.0 / math.sqrt(2.0))))
    density = jnp.exp(-0.5 * inner * inner) * (1.0 / math.sqrt(2.0 * math.pi))
    return inner * phi, phi + inner * density


def rows_to_columns(rows):
    pad = -rows.shape[0] % 8
    if pad:
        rows = jnp.concatenate([rows, jnp.zeros((pad, LANES), F32)], 0)
    return rows.T


def times_columns(cols, count, w_ref, e, lanes):
    wide = [jnp.broadcast_to(cols[:, i : i + 1], (LANES, LANES)) for i in range(count)]
    rows = []
    for j in range(lanes):
        acc = None
        for i in range(count):
            term = wide[i] * w_ref[e, LANES * i : LANES * (i + 1), LANES * j : LANES * (j + 1)]
            term = jnp.sum(term.reshape(LANES // 8, 8, LANES), 0)
            acc = term if acc is None else acc + term
        rows.append(jnp.sum(acc, 0, keepdims=True))
    return jnp.concatenate(rows, 0)


def times_rows(rows, count, w_ref, e, blocks):
    out = []
    for i in range(blocks):
        acc = None
        for j in range(count):
            term = rows[j : j + 1] * w_ref[e, LANES * i : LANES * (i + 1), LANES * j : LANES * (j + 1)]
            acc = term if acc is None else acc + term
        out.append(jnp.sum(acc.T, 0, keepdims=True))
    return jnp.concatenate(out, 0)


def expert_kernel(n_dp, n_ex, stats_ref, win_hbm, bin_ref, wdown_hbm, bdown_ref, shared_ref, own_ref, inner_ref,
                  win, wdown, near, mine, far, send_near, recv_near, send_far, recv_far, send_out, recv_out, got, loads):
    dp, ex = lax.axis_index("dp"), lax.axis_index("expert")
    owned = win.shape[0]
    barrier = pltpu.get_barrier_semaphore()
    for i in range(1, n_ex):
        pl.semaphore_signal(barrier, inc=1, device_id=(dp, lax.rem(ex + i, n_ex)), device_id_type=MESH)
    for i in range(1, n_dp):
        pl.semaphore_signal(barrier, inc=1, device_id=(lax.rem(dp + i, n_dp), ex), device_id_type=MESH)
    load_in = pltpu.make_async_copy(win_hbm, win, loads.at[0])
    load_in.start()
    load_down = pltpu.make_async_copy(wdown_hbm, wdown, loads.at[1])
    load_down.start()
    pl.semaphore_wait(barrier, n_ex + n_dp - 2)
    copies = []
    for i in range(1, n_ex):
        to = lax.rem(ex + i, n_ex)
        copy = pltpu.make_async_remote_copy(
            src_ref=stats_ref.at[pl.ds(to * owned, owned)], dst_ref=near.at[i - 1], send_sem=send_near.at[i - 1],
            recv_sem=recv_near.at[i - 1], device_id=(dp, to), device_id_type=MESH)
        copy.start()
        copies.append(copy)
    for copy in copies:
        copy.wait()
    mine[...] = merge([stats_ref[pl.ds(ex * owned, owned)]] + [near[i] for i in range(n_ex - 1)])
    copies = []
    for i in range(1, n_dp):
        to = lax.rem(dp + i, n_dp)
        copy = pltpu.make_async_remote_copy(
            src_ref=mine, dst_ref=far.at[i - 1], send_sem=send_far.at[i - 1], recv_sem=recv_far.at[i - 1],
            device_id=(to, ex), device_id_type=MESH)
        copy.start()
        copies.append(copy)
    for copy in copies:
        copy.wait()
    tiles = merge([mine[...]] + [far[i] for i in range(n_dp - 1)])
    load_in.wait()
    load_down.wait()
    blocks, wide = win.shape[1] // LANES, win.shape[2] // LANES
    for e in range(owned):
        tile = tiles[e]
        slots = tile[0:blocks] / tile[7:8]
        d_out = tile[3 : 3 + blocks]
        bias = jnp.concatenate([bin_ref[e : e + 1, LANES * j : LANES * (j + 1)] for j in range(wide)], 0)
        inner = times_columns(rows_to_columns(slots), blocks, win, e, wide) + bias
        hidden, slope = gelu_parts(inner)
        bias = jnp.concatenate([bdown_ref[e : e + 1, LANES * j : LANES * (j + 1)] for j in range(blocks)], 0)
        out = times_columns(rows_to_columns(hidden), wide, wdown, e, blocks) + bias
        d_inner = times_rows(d_out, blocks, wdown, e, wide) * slope
        d_slots = times_rows(d_inner, wide, win, e, blocks)
        along = jnp.sum(slots * d_slots, keepdims=True)
        lane = lax.broadcasted_iota(jnp.int32, (1, LANES), 1)
        last = jnp.where(lane < LANES // 2, tile[7:8], along)
        shared_ref[ex * owned + e] = jnp.concatenate([out, d_slots, tile[6:7], last], 0)
        own_ref[e] = jnp.concatenate([slots, d_out, jnp.zeros((2, LANES), F32)], 0)
        got[e] = jnp.concatenate([out, d_slots, tile[6:7], last], 0)
        inner_ref[e] = jnp.concatenate([hidden, d_inner], 0)
    copies = []
    for i in range(1, n_ex):
        to = lax.rem(ex + i, n_ex)
        copy = pltpu.make_async_remote_copy(
            src_ref=got, dst_ref=shared_ref.at[pl.ds(ex * owned, owned)], send_sem=send_out.at[i - 1],
            recv_sem=recv_out.at[i - 1], device_id=(dp, to), device_id_type=MESH)
        copy.start()
        copies.append(copy)
    for copy in copies:
        copy.wait()


def norm_back(grad, hat, scale, gain):
    g = grad * gain
    return scale * (g - jnp.mean(g, -1, keepdims=True) - hat * jnp.mean(g * hat, -1, keepdims=True))


def back_kernel(x_ref, live_ref, g1_ref, b1_ref, wqkv_ref, wout_ref, g2_ref, b2_ref, keys_ref, cot_ref, resid_ref,
                joined_ref, context_ref, attn_ref, logits_ref, shared_ref, own_ref, inner_ref,
                act_ref, gx_ref, gwqkv_ref, gwout_ref, small_ref, gwin_hbm, gwdown_hbm, gin, gdown, djoined_ref, sems):
    length, width = resid_ref.shape
    owned = own_ref.shape[0]
    blocks = width // LANES
    wide = gin.shape[2] // LANES
    writes = []
    for e in range(owned):
        slot_cols = rows_to_columns(own_ref[e])
        hidden_cols = rows_to_columns(inner_ref[e])
        for i in range(blocks):
            col = jnp.broadcast_to(slot_cols[:, i : i + 1], (LANES, LANES))
            for j in range(wide):
                gin[e, LANES * i : LANES * (i + 1), LANES * j : LANES * (j + 1)] = col * inner_ref[e, wide + j : wide + j + 1]
        copy = pltpu.make_async_copy(gin.at[e], gwin_hbm.at[e], sems.at[2 * e])
        copy.start()
        writes.append(copy)
        for j in range(wide):
            col = jnp.broadcast_to(hidden_cols[:, j : j + 1], (LANES, LANES))
            for i in range(blocks):
                gdown[e, LANES * j : LANES * (j + 1), LANES * i : LANES * (i + 1)] = col * own_ref[e, 3 + i : 4 + i]
        copy = pltpu.make_async_copy(gdown.at[e], gwdown_hbm.at[e], sems.at[2 * e + 1])
        copy.start()
        writes.append(copy)
    shared = shared_ref[...]
    slot_out = from_tiles(shared, 0, 3)
    d_slots = from_tiles(shared, 3, 3)
    peak = shared[:, 6, 0:1]
    total = shared[:, 7, 0:1]
    along = shared[:, 7, LANES - 1 : LANES]
    cot = cot_ref[0]
    resid = resid_ref[...]
    hat2, scale2 = norm_stats(resid)
    normed2 = hat2 * g2_ref[...] + b2_ref[...]
    logits = logits_ref[...]
    dispatch = jnp.exp(jnp.where(live_ref[...] > 0, logits, NEGATIVE) - peak) / total
    comb = jnp.exp(logits - jnp.max(logits, 0, keepdims=True))
    comb = comb * (1.0 / jnp.sum(comb, 0, keepdims=True))
    act_ref[0] = resid + dot(comb, slot_out, 0, 0)
    d_comb = dot(slot_out, cot, 1, 1)
    d_logits = comb * (d_comb - jnp.sum(comb * d_comb, 0, keepdims=True))
    d_logits = d_logits + dispatch * (dot(d_slots, normed2, 1, 1) - along)
    d_normed2 = dot(jnp.concatenate([dispatch, d_logits], 0), jnp.concatenate([d_slots, keys_ref[...].T], 0), 0, 0)
    small_ref[8:16] = dot(d_logits, normed2, 1, 0)
    small_ref[5:6] = jnp.sum(d_normed2 * hat2, 0, keepdims=True)
    small_ref[6:7] = jnp.sum(d_normed2, 0, keepdims=True)
    d_resid = cot + norm_back(d_normed2, hat2, scale2, g2_ref[...])
    context = context_ref[...]
    gwout_ref[...] = dot(context, d_resid, 1, 0)
    small_ref[4:5] = jnp.sum(d_resid, 0, keepdims=True)
    d_context = dot(wout_ref[...], d_resid, 1, 1)
    along_q = d_context * context
    scale = 1.0 / math.sqrt(HEAD_DIM)
    half = length // 2
    for h in range(HEADS):
        at = HEAD_DIM * h
        span = slice(at, at + HEAD_DIM)
        q_hi, q_lo = parts(joined_ref[at : at + HEAD_DIM])
        k_hi, k_lo = parts(joined_ref[width + at : width + at + HEAD_DIM])
        v_hi, v_lo = parts(joined_ref[2 * width + at : 2 * width + at + HEAD_DIM])
        o_hi, o_lo = parts(d_context[span])
        rowsum = jnp.sum(along_q[span], 0, keepdims=True)
        values = jnp.concatenate([v_hi, v_lo, v_hi], 0).T
        d_out = jnp.concatenate([o_hi, o_hi, o_lo], 0)
        keys = jnp.concatenate([k_hi, k_lo], 0)
        queries = jnp.concatenate([q_hi, q_lo], 0)
        outs = jnp.concatenate([o_hi, o_lo], 0)
        d_v = d_k = None
        for b in range(2):
            part = slice(half * b, half * (b + 1))
            attn = attn_ref[h, :, part]
            d_attn = dot(values, d_out[:, part], 1, 0, None)
            d_scores = attn * (d_attn - rowsum[:, part])
            p_hi, p_lo = parts(attn)
            s_hi, s_lo = parts(d_scores)
            both = dot(keys, s_hi, 1, 0, None)
            d_q = both[:HEAD_DIM] + both[HEAD_DIM:] + dot(k_hi, s_lo, 1, 0, None)
            djoined_ref[span, part] = d_q * scale
            both = dot(outs[:, part], p_hi, 1, 1, None)
            term = both[:HEAD_DIM] + both[HEAD_DIM:] + dot(o_hi[:, part], p_lo, 1, 1, None)
            d_v = term if d_v is None else d_v + term
            both = dot(queries[:, part], s_hi, 1, 1, None)
            term = both[:HEAD_DIM] + both[HEAD_DIM:] + dot(q_hi[:, part], s_lo, 1, 1, None)
            d_k = term if d_k is None else d_k + term
        djoined_ref[width + at : width + at + HEAD_DIM] = d_k
        djoined_ref[2 * width + at : 2 * width + at + HEAD_DIM] = d_v
    d_joined = djoined_ref[...]
    x = x_ref[0]
    hat, scale1 = norm_stats(x)
    normed = hat * g1_ref[...] + b1_ref[...]
    gwqkv_ref[...] = dot(normed, d_joined, 0, 1)
    sums = dot(jnp.ones((8, length), F32), d_joined, 1, 1)
    small_ref[2:3] = sums[0:1, :width]
    small_ref[3:4] = sums[0:1, 2 * width :]
    d_normed = dot(d_joined, wqkv_ref[...], 0, 1)
    small_ref[0:1] = jnp.sum(d_normed * hat, 0, keepdims=True)
    small_ref[1:2] = jnp.sum(d_normed, 0, keepdims=True)
    small_ref[7:8] = jnp.zeros((1, width), F32)
    gx_ref[0] = d_resid + norm_back(d_normed, hat, scale1, g1_ref[...])
    for copy in writes:
        copy.wait()


def sds(*shape):
    return jax.ShapeDtypeStruct(shape, F32)


def solution(mesh):
    n_dp, n_ex = mesh.shape["dp"], mesh.shape["expert"]

    def on_device(patches, image_ids, pad_mask, ln1_gain, ln1_bias, w_qkv, bias_qv, w_out, bias_out, ln2_gain, ln2_bias,
                  slot_keys, w_in, bias_in, w_down, bias_down, cotangent):
        _, length, width = patches.shape
        owned, _, hidden = w_in.shape
        experts = owned * n_ex
        row = lambda v: v.reshape(1, -1)
        g1, b1, bo, g2, b2 = map(row, (ln1_gain, ln1_bias, bias_out, ln2_gain, ln2_bias))
        resid, joined, context, attn, logits, stats = pl.pallas_call(
            front_kernel,
            out_shape=(sds(length, width), sds(3 * width, length), sds(width, length), sds(HEADS, length, length),
                       sds(experts, length), sds(experts, 8, LANES)),
            in_specs=[VMEM] * 13,
            out_specs=[VMEM] * 6,
            scratch_shapes=[pltpu.VMEM((length, length), F32)],
            compiler_params=pltpu.CompilerParams(vmem_limit_bytes=40 << 20),
            name="front",
        )(patches, image_ids, pad_mask, g1, b1, w_qkv, bias_qv, w_out, bo, g2, b2, slot_keys, cotangent)
        shared, own, inner = pl.pallas_call(
            functools.partial(expert_kernel, n_dp, n_ex),
            out_shape=(sds(experts, 8, LANES), sds(owned, 8, LANES), sds(owned, 2 * hidden // LANES, LANES)),
            in_specs=[VMEM, ANY, VMEM, ANY, VMEM],
            out_specs=[VMEM] * 3,
            scratch_shapes=[
                pltpu.VMEM(w_in.shape, F32), pltpu.VMEM(w_down.shape, F32),
                pltpu.VMEM((n_ex - 1, owned, 8, LANES), F32), pltpu.VMEM((owned, 8, LANES), F32),
                pltpu.VMEM((n_dp - 1, owned, 8, LANES), F32),
                pltpu.SemaphoreType.DMA((n_ex - 1,)), pltpu.SemaphoreType.DMA((n_ex - 1,)),
                pltpu.SemaphoreType.DMA((n_dp - 1,)), pltpu.SemaphoreType.DMA((n_dp - 1,)),
                pltpu.SemaphoreType.DMA((n_ex - 1,)), pltpu.SemaphoreType.DMA((n_ex - 1,)),
                pltpu.VMEM((owned, 8, LANES), F32), pltpu.SemaphoreType.DMA((2,)),
            ],
            compiler_params=pltpu.CompilerParams(collective_id=0, has_side_effects=True, vmem_limit_bytes=24 << 20),
            name="experts",
        )(stats, w_in, bias_in, w_down, bias_down)
        act, gx, gwqkv, gwout, small, gwin, gwdown = pl.pallas_call(
            back_kernel,
            out_shape=(sds(1, length, width), sds(1, length, width), sds(*w_qkv.shape), sds(*w_out.shape), sds(16, width),
                       sds(*w_in.shape), sds(*w_down.shape)),
            in_specs=[VMEM] * 18,
            out_specs=[VMEM] * 5 + [ANY] * 2,
            scratch_shapes=[pltpu.VMEM(w_in.shape, F32), pltpu.VMEM(w_down.shape, F32), pltpu.VMEM((3 * width, length), F32),
                            pltpu.SemaphoreType.DMA((2 * owned,))],
            compiler_params=pltpu.CompilerParams(vmem_limit_bytes=56 << 20),
            name="back",
        )(patches, pad_mask, g1, b1, w_qkv, w_out, g2, b2, slot_keys, cotangent, resid, joined, context, attn, logits,
          shared, own, inner)
        gwqkv, gwout, small = lax.psum((gwqkv, gwout, small), ("dp", "expert"))
        flat = lambda i: small[i].reshape(width)
        d_inner = inner[:, hidden // LANES :].reshape(owned, hidden)
        d_out = own[:, 3 : 3 + width // LANES].reshape(owned, width)
        return (act, gx, flat(0), flat(1), gwqkv, small[2:4], gwout, flat(4), flat(5), flat(6), small[8:16].T, gwin, d_inner,
                gwdown, d_out)

    rows = P(("dp", "expert"), None, None)
    flags = P(("dp", "expert"), None)
    e3, e2 = P("expert", None, None), P("expert", None)
    return jax.shard_map(
        on_device,
        mesh=mesh,
        in_specs=(rows, flags, flags) + (P(),) * 9 + (e3, e2, e3, e2, rows),
        out_specs=(rows, rows) + (P(),) * 9 + (e3, e2, e3, e2),
        check_vma=False,
    )
```

profile of v0, /device:TPU:0, one launch (start us, length us, event | category | flops | bytes accessed | tf_op | source)
XLA Modules:
  0.0 230.3 jit_solution(4520513019899382461)
XLA Ops:
  7.2 0.0 all-reduce.3.cloned.1.call-start
  7.2 0.8 copy.35.keys_ref
  8.1 0.0 copy-start.8
  8.1 0.7 reshape.51.g1_ref
  8.8 0.7 reshape.52.b1_ref
  9.5 0.7 reshape.53.g2_ref
  10.2 0.7 reshape.54.b2_ref
  10.8 0.7 reshape.55.bout_ref
  11.5 1.5 copy-done
  13.0 1.1 copy-done.4
  14.1 1.1 copy-done.5
  15.3 1.1 copy-done.6
  16.3 0.7 copy-done.22
  17.0 0.7 copy-done.23
  17.7 0.7 copy-done.25
  18.4 11.3 %front.1 = (f32[512,384]{1,0:T(8,128)S(1)}, f32[1152,512]{1,0:T(8,128)S(1)}, f32[384,512]{1,0:T(8,128)S(1)}, f32[6,512,512]{2,1,0:T(8,128)S(1)}, f32[8,512]{1,0:T(8,128)S(1)}, /*index=5*/f32[8,8,128]{2,1,0:T(8,128)S(1)}) custom-call(f32[1,512,384]{2,1,0:T(8,128)S(1)} %copy-done.4, s32[1,512]{1,0:T(1,128)S(1)} %copy-done.25, s32[1,512]{1,0:T(1,128)S(1)} %copy-done.22, ...), custom_call_target="tpu_custom_call" | custom-call | tf_op jit(solution)/shard_map/front/pallas_call | solution.py:348
  29.7 0.0 copy-start.10
  29.7 0.9 copy-done.10
  30.6 0.0 copy-start.2
  30.7 5.7 %copy-done.2 = f32[2,384,1536]{2,1,0:T(8,128)S(1)} copy-done((f32[2,384,1536]{2,1,0:T(8,128)S(1)}, f32[2,384,1536]{2,1,0:T(8,128)}, u32[]{:S(2)}) %copy-start.2) | copy-done | bytes 4718616
  36.3 2.3 %copy-done.3 = f32[2,1536,384]{2,1,0:T(8,128)S(1)} copy-done((f32[2,1536,384]{2,1,0:T(8,128)S(1)}, f32[2,1536,384]{2,1,0:T(8,128)}, u32[]{:S(2)}) %copy-start.3) | copy-done | bytes 4718616
  38.7 0.7 copy-done.21
  39.4 0.7 copy-done.24
  40.0 17.2 %experts.1 = (f32[8,8,128]{2,1,0:T(8,128)S(1)}, f32[2,8,128]{2,1,0:T(8,128)S(1)}, f32[2,24,128]{2,1,0:T(8,128)S(1)}) custom-call(f32[8,8,128]{2,1,0:T(8,128)S(1)} %get-tuple-element.36.stats_ref, f32[2,384,1536]{2,1,0:T(8,128)S(1)} %copy-done.2, f32[2,1536]{1,0:T(2,128)S(1)} %copy-done.21, f32[2,1536,384]{2,1,0:T(8,128)S(1)} %copy-done.3, ...), custom_call_target="tpu_custom_call" | custom-call | tf_op jit(solution)/shard_map/experts/pallas_call | solution.py:358
  57.2 0.0 copy-done.8
  57.2 0.0 copy-done.17
  57.3 0.0 copy-done.18
  57.3 0.0 copy-done.19
  57.3 0.0 copy-done.20
  57.3 0.0 copy-done.1
  57.3 0.0 copy-done.7
  57.3 0.0 copy-done.9
  57.3 0.0 copy-done.16
  57.3 0.6 copy-done.11
  57.9 0.6 copy-done.13
  58.5 0.6 copy-done.14
  59.1 23.0 %back.1 = (f32[1,512,384]{2,1,0:T(8,128)}, f32[1,512,384]{2,1,0:T(8,128)}, f32[384,1152]{1,0:T(8,128)}, f32[384,384]{1,0:T(8,128)}, f32[16,384]{1,0:T(8,128)}, /...) custom-call(f32[1,512,384]{2,1,0:T(8,128)} %x_ref.3, s32[1,512]{1,0:T(1,128)} %live_ref.3, f32[1,384]{1,0:T(1,128)} %copy-done.17, ...), custom_call_target="tpu_custom_call" | custom-call | tf_op jit(solution)/shard_map/back/pallas_call | solution.py:375
  82.2 0.0 all-reduce.3.cloned.1.call-update
  82.2 40.2 %psum.21 = f32[16,384]{1,0:T(8,128)S(1)} all-reduce(f32[16,384]{1,0:T(8,128)} %get-tuple-element.42), channel_id=1, replica_groups=mesh['dp'=8,'expert'=4] {'dp','expert'}, use_global_device_ids=true, to_apply=%region_0.0 | all-reduce | flops 6144 | bytes 49152 | tf_op jit(solution)/shard_map/psum | solution.py:387
  122.4 0.6 slice.38
  123.0 0.0 copy-done.12
  123.0 0.6 copy.40
  123.6 0.6 copy.41
  124.2 0.6 slice_reduce_fusion
  124.8 0.6 slice_bitcast_fusion.1
  125.4 93.3 %all-reduce.3.cloned.1.call-done = (f32[384,1152]{1,0:T(8,128)}, f32[384,384]{1,0:T(8,128)}) async-done(((f32[384,1152]{1,0:T(8,128)}, f32[384,384]{1,0:T(8,128)}), (f32[384,1152]{1,0:T(8,128)}, f32[384,384]{1,0:T(8,128)})) %all-reduce.3.cloned.1.call-update) | async-done | bytes 2359312 | tf_op jit(solution)/shard_map/psum | solution.py:387
  218.7 2.8 %copy.44 = f32[384,1152]{1,0:T(8,128)} copy(f32[384,1152]{1,0:T(8,128)} %get-tuple-element.58) | data formatting | bytes 3538944
  221.5 1.9 copy.45
  (26 shorter events, 0.0 us)
Async XLA Ops:
  7.2 211.5 %all-reduce.3.cloned.1.call-start = ((), (), s32[]{:S(2)}) async-start(), calls=%async_computation | async-start | bytes 4718592 | tf_op jit(solution)/shard_map/psum | solution.py:387
  8.1 49.2 %copy-start.8 = (f32[384,8]{1,0:T(8,128)}, f32[384,8]{1,0:T(8,128)S(1)}, u32[]{:S(2)}) copy-start(f32[384,8]{1,0:T(8,128)S(1)} %copy.35.keys_ref) | copy-start | bytes 36868
  8.8 48.5 %copy-start.17 = (f32[1,384]{1,0:T(1,128)}, f32[1,384]{1,0:T(1,128)S(1)}, u32[]{:S(2)}) copy-start(f32[1,384]{1,0:T(1,128)S(1)} %reshape.51.g1_ref) | copy-start | bytes 4612
  9.5 47.8 %copy-start.18 = (f32[1,384]{1,0:T(1,128)}, f32[1,384]{1,0:T(1,128)S(1)}, u32[]{:S(2)}) copy-start(f32[1,384]{1,0:T(1,128)S(1)} %reshape.52.b1_ref) | copy-start | bytes 4612
  10.2 47.1 %copy-start.19 = (f32[1,384]{1,0:T(1,128)}, f32[1,384]{1,0:T(1,128)S(1)}, u32[]{:S(2)}) copy-start(f32[1,384]{1,0:T(1,128)S(1)} %reshape.53.g2_ref) | copy-start | bytes 4612
  10.8 46.4 %copy-start.20 = (f32[1,384]{1,0:T(1,128)}, f32[1,384]{1,0:T(1,128)S(1)}, u32[]{:S(2)}) copy-start(f32[1,384]{1,0:T(1,128)S(1)} %reshape.54.b2_ref) | copy-start | bytes 4612
  11.5 1.5 copy-start
  13.0 1.1 copy-start.4
  14.1 1.1 copy-start.5
  15.3 1.1 copy-start.6
  16.3 0.7 copy-start.22
  17.0 0.7 copy-start.23
  17.7 0.7 copy-start.25
  29.7 0.9 copy-start.10
  30.6 26.6 %copy-start.1 = (f32[6,512,512]{2,1,0:T(8,128)}, f32[6,512,512]{2,1,0:T(8,128)S(1)}, u32[]{:S(2)}) copy-start(f32[6,512,512]{2,1,0:T(8,128)S(1)} %get-tuple-element.34.attn_ref) | copy-start | bytes 18874372
  30.6 26.7 %copy-start.7 = (f32[1152,512]{1,0:T(8,128)}, f32[1152,512]{1,0:T(8,128)S(1)}, u32[]{:S(2)}) copy-start(f32[1152,512]{1,0:T(8,128)S(1)} %get-tuple-element.32.joined_ref) | copy-start | bytes 7077892
  30.6 26.7 %copy-start.9 = (f32[512,384]{1,0:T(8,128)}, f32[512,384]{1,0:T(8,128)S(1)}, u32[]{:S(2)}) copy-start(f32[512,384]{1,0:T(8,128)S(1)} %get-tuple-element.31.resid_ref) | copy-start | bytes 2359300
  30.6 26.7 %copy-start.16 = (f32[8,512]{1,0:T(8,128)}, f32[8,512]{1,0:T(8,128)S(1)}, u32[]{:S(2)}) copy-start(f32[8,512]{1,0:T(8,128)S(1)} %get-tuple-element.35.logits_ref) | copy-start | bytes 49156
  30.6 5.7 %copy-start.2 = (f32[2,384,1536]{2,1,0:T(8,128)S(1)}, f32[2,384,1536]{2,1,0:T(8,128)}, u32[]{:S(2)}) copy-start(f32[2,384,1536]{2,1,0:T(8,128)} %win_hbm.1) | copy-start | bytes 14155780
  36.3 2.3 %copy-start.3 = (f32[2,1536,384]{2,1,0:T(8,128)S(1)}, f32[2,1536,384]{2,1,0:T(8,128)}, u32[]{:S(2)}) copy-start(f32[2,1536,384]{2,1,0:T(8,128)} %wdown_hbm.1) | copy-start | bytes 14155780
  38.7 0.7 copy-start.21
  39.4 0.7 copy-start.24
  57.3 0.6 copy-start.11
  57.9 0.6 copy-start.13
  58.5 0.6 copy-start.14
  59.1 63.9 %copy-start.12 = (f32[2,24,128]{2,1,0:T(8,128)S(1)}, f32[2,24,128]{2,1,0:T(8,128)}, u32[]{:S(2)}) copy-start(f32[2,24,128]{2,1,0:T(8,128)} %copy-done.11) | copy-start | bytes 73732
  59.1 64.5 %copy-start.15 = (f32[2,8,128]{2,1,0:T(8,128)S(1)}, f32[2,8,128]{2,1,0:T(8,128)}, u32[]{:S(2)}) copy-start(f32[2,8,128]{2,1,0:T(8,128)} %copy-done.14) | copy-start | bytes 24580
Sparse Core Ops, SparseCore 0:
  82.3 136.3 all-reduce.2
where the time goes:
time: 231 us; the launch traced here: 230 us
  waiting for transfers between devices  93.3 us (40%)
  Pallas kernels  51.5 us (22%)
  blocking collectives  40.2 us (17%)
  local copies, waits for them, and re-layouts  31 us (13%)
  between operations  14.2 us (6%)
    psum x1, waiting for transfers between devices, on_device(): gwqkv, gwout, small = lax.psum((gwqkv, gwout, small), ('dp', 'expert'))  93.3 us
    psum x1, blocking collectives, on_device(): gwqkv, gwout, small = lax.psum((gwqkv, gwout, small), ('dp', 'expert'))  40.2 us
    unnamed x59, local copies, waits for them, and re-layouts  25.7 us
    pallas_call x1, Pallas kernels, on_device(): pl.pallas_call(back_kernel, out_shape=(sds(1, length, width), sds(1, leng...  23 us
    pallas_call x1, Pallas kernels, on_device(): pl.pallas_call(functools.partial(expert_kernel, n_dp, n_ex), out_shape=(s...  17.2 us
    pallas_call x1, Pallas kernels, on_device(): pl.pallas_call(front_kernel, out_shape=(sds(length, width), sds(3 * width...  11.3 us
  transfers between devices with their start and end apart: 1, of which 1 were waited for; matrix products, arithmetic and copies ran while one was open for 1% of the time, Pallas kernels for 0%

commit v1 on v0

v1 whole, which is shorter than its diff:
```python
import functools
import math

import jax
import jax.numpy as jnp
from jax import lax
from jax.experimental import pallas as pl
from jax.experimental.pallas import tpu as pltpu
from jax.sharding import PartitionSpec as P

HEADS = 6
HEAD_DIM = 64
LANES = 128
EPSILON = 1e-06
NEGATIVE = -1e30
HIGH = lax.Precision.HIGH
BF = jnp.bfloat16
F32 = jnp.float32
MESH = pl.DeviceIdType.MESH
FRONT_VMEM = ROUTE_VMEM = BACK_VMEM = 60 << 20
FINISH_VMEM = 8 << 20
VMEM = pl.BlockSpec(memory_space=pltpu.VMEM)
ANY = pl.BlockSpec(memory_space=pl.ANY)


def dot(left, right, dim_left, dim_right, precision=HIGH):
    return lax.dot_general(
        left, right, (((dim_left,), (dim_right,)), ((), ())), precision=precision, preferred_element_type=F32
    )


def parts(value):
    high = value.astype(BF)
    return high, (value - high.astype(F32)).astype(BF)


def norm_stats(values):
    center = values - jnp.mean(values, -1, keepdims=True)
    spread = jnp.mean(center * center, -1, keepdims=True)
    scale = lax.rsqrt(spread + EPSILON)
    return center * scale, scale


def column(row):
    return jnp.broadcast_to(row, (8, row.shape[1])).T[:, :1]


def load(sources, targets, sems):
    copies = [pltpu.make_async_copy(src, dst, sems.at[i]) for i, (src, dst) in enumerate(zip(sources, targets))]
    for copy in copies:
        copy.start()
    return copies


def greet(n_dp, n_ex, dp, ex):
    barrier = pltpu.get_barrier_semaphore()
    for i in range(1, n_ex):
        pl.semaphore_signal(barrier, inc=1, device_id=(dp, lax.rem(ex + i, n_ex)), device_id_type=MESH)
    for i in range(1, n_dp):
        pl.semaphore_signal(barrier, inc=1, device_id=(lax.rem(dp + i, n_dp), ex), device_id_type=MESH)
    return lambda: pl.semaphore_wait(barrier, n_ex + n_dp - 2)


def send(src, dst, out_sem, in_sem, dp, ex):
    copy = pltpu.make_async_remote_copy(
        src_ref=src, dst_ref=dst, send_sem=out_sem, recv_sem=in_sem, device_id=(dp, ex), device_id_type=MESH)
    copy.start()
    return copy


def as_row(ref):
    return ref[...].reshape(1, -1)


def to_tiles(rows):
    return jnp.stack([jnp.concatenate([rows[e : e + 1, LANES * i : LANES * (i + 1)] for i in range(8)], 0) for e in range(rows.shape[0])], 0)


def from_tiles(tiles, first, count):
    return jnp.concatenate([tiles[:, first + i, :] for i in range(count)], -1)


def merge(tiles):
    peaks = [tile[:, 6:7, :] for tile in tiles]
    peak = functools.reduce(jnp.maximum, peaks)
    row = lax.broadcasted_iota(jnp.int32, tiles[0].shape, 1)
    weighted = (row < 3) | (row == 7)
    total = None
    for tile, own in zip(tiles, peaks):
        scaled = jnp.where(weighted, tile * jnp.exp(own - peak), tile)
        total = scaled if total is None else total + scaled
    return jnp.where(row == 6, peak, total)


def gelu_parts(inner):
    phi = 0.5 * (1.0 + lax.erf(inner * (1.0 / math.sqrt(2.0))))
    density = jnp.exp(-0.5 * inner * inner) * (1.0 / math.sqrt(2.0 * math.pi))
    return inner * phi, phi + inner * density


def rows_to_columns(rows):
    pad = -rows.shape[0] % 8
    if pad:
        rows = jnp.concatenate([rows, jnp.zeros((pad, LANES), F32)], 0)
    return rows.T


def times_columns(cols, count, w_ref, e, lanes):
    wide = [jnp.broadcast_to(cols[:, i : i + 1], (LANES, LANES)) for i in range(count)]
    rows = []
    for j in range(lanes):
        acc = None
        for i in range(count):
            term = wide[i] * w_ref[e, LANES * i : LANES * (i + 1), LANES * j : LANES * (j + 1)]
            term = jnp.sum(term.reshape(LANES // 8, 8, LANES), 0)
            acc = term if acc is None else acc + term
        rows.append(jnp.sum(acc, 0, keepdims=True))
    return jnp.concatenate(rows, 0)


def times_rows(rows, count, w_ref, e, blocks):
    out = []
    for i in range(blocks):
        acc = None
        for j in range(count):
            term = rows[j : j + 1] * w_ref[e, LANES * i : LANES * (i + 1), LANES * j : LANES * (j + 1)]
            acc = term if acc is None else acc + term
        out.append(jnp.sum(acc.T, 0, keepdims=True))
    return jnp.concatenate(out, 0)


def front_kernel(n_dp, n_ex, x_in, ids_in, live_in, g1_in, b1_in, wqkv_in, bqv_in, wout_in, bout_in, g2_in, b2_in, keys_in,
                 cot_in, win_in, bin_in, wdown_in, bdown_in,
                 resid_out, joined_out, context_out, attn_out, logits_out, shared_out, own_out, inner_out,
                 x_ref, ids_ref, live_ref, g1_ref, b1_ref, wqkv_ref, bqv_ref, wout_ref, bout_ref, g2_ref, b2_ref, keys_ref,
                 cot_ref, win, bin_ref, wdown, bdown_ref,
                 resid_ref, joined_ref, context_ref, attn_ref, logits_ref, block_ref,
                 stats_ref, near, mine, far, got, shared_ref, own_ref, inner_ref,
                 loads, stores, send_near, recv_near, send_far, recv_far, send_out, recv_out):
    dp, ex = lax.axis_index("dp"), lax.axis_index("expert")
    owned = win.shape[0]
    all_here = greet(n_dp, n_ex, dp, ex)
    coming = load(
        (x_in, g1_in, b1_in, wqkv_in, bqv_in, ids_in, wout_in, bout_in, g2_in, b2_in, keys_in, live_in, cot_in, win_in, bin_in,
         wdown_in, bdown_in),
        (x_ref, g1_ref, b1_ref, wqkv_ref, bqv_ref, ids_ref, wout_ref, bout_ref, g2_ref, b2_ref, keys_ref, live_ref, cot_ref, win,
         bin_ref, wdown, bdown_ref), loads)
    going = []

    def keep(src, dst):
        copy = pltpu.make_async_copy(src, dst, stores.at[len(going)])
        copy.start()
        going.append(copy)

    for copy in coming[:3]:
        copy.wait()
    x = x_ref[0]
    length, width = x.shape
    hat, _ = norm_stats(x)
    normed = hat * as_row(g1_ref) + as_row(b1_ref)
    for copy in coming[3:6]:
        copy.wait()
    joined = dot(wqkv_ref[...], normed, 0, 1)
    bias = jnp.broadcast_to(bqv_ref[0:1], (8, width)).T[:, :1]
    bias_v = jnp.broadcast_to(bqv_ref[1:2], (8, width)).T[:, :1]
    scale = 1.0 / math.sqrt(HEAD_DIM)
    joined_ref[0:width] = (joined[:width] + bias) * scale
    joined_ref[width : 2 * width] = joined[width : 2 * width]
    joined_ref[2 * width :] = joined[2 * width :] + bias_v
    keep(joined_ref, joined_out)
    ids = ids_ref[...].astype(F32)
    block_ref[...] = jnp.where(column(ids) == ids, 0.0, NEGATIVE)
    half = length // 2
    for h in range(HEADS):
        at = HEAD_DIM * h
        q_hi, q_lo = parts(joined_ref[at : at + HEAD_DIM])
        k_hi, k_lo = parts(joined_ref[width + at : width + at + HEAD_DIM])
        v_hi, v_lo = parts(joined_ref[2 * width + at : 2 * width + at + HEAD_DIM])
        queries = jnp.concatenate([q_hi, q_hi, q_lo], 0)
        keys = jnp.concatenate([k_hi, k_lo, k_hi], 0).T
        values = jnp.concatenate([v_hi, v_lo], 0)
        for b in range(2):
            span = slice(half * b, half * (b + 1))
            scores = dot(keys, queries[:, span], 1, 0, None) + block_ref[:, span]
            expo = jnp.exp(scores - jnp.max(scores, 0, keepdims=True))
            attn = expo * (1.0 / jnp.sum(expo, 0, keepdims=True))
            attn_ref[h, :, span] = attn
            p_hi, p_lo = parts(attn)
            both = dot(values, p_hi, 1, 0, None)
            context_ref[at : at + HEAD_DIM, span] = both[:HEAD_DIM] + both[HEAD_DIM:] + dot(v_hi, p_lo, 1, 0, None)
        keep(attn_ref.at[h], attn_out.at[h])
    keep(context_ref, context_out)
    for copy in coming[6:13]:
        copy.wait()
    resid = x + dot(context_ref[...], wout_ref[...], 0, 0) + as_row(bout_ref)
    resid_ref[...] = resid
    keep(resid_ref, resid_out)
    hat2, _ = norm_stats(resid)
    normed2 = hat2 * as_row(g2_ref) + as_row(b2_ref)
    logits = dot(keys_ref[...], normed2, 1, 1)
    logits_ref[...] = logits
    keep(logits_ref, logits_out)
    masked = jnp.where(live_ref[...] > 0, logits, NEGATIVE)
    peak = jnp.max(masked, 1, keepdims=True)
    expo = jnp.exp(masked - peak)
    total = jnp.sum(expo, 1, keepdims=True)
    summed = dot(expo, normed2, 1, 0)
    top = jnp.max(logits, 0, keepdims=True)
    comb = jnp.exp(logits - top)
    comb = comb * (1.0 / jnp.sum(comb, 0, keepdims=True))
    part_out = dot(comb, cot_ref[0], 1, 0)
    experts = logits.shape[0]
    stats_ref[...] = to_tiles(jnp.concatenate(
        [summed, part_out, jnp.broadcast_to(peak, (experts, LANES)), jnp.broadcast_to(total, (experts, LANES))], 1))
    all_here()
    copies = []
    for i in range(1, n_ex):
        to = lax.rem(ex + i, n_ex)
        copies.append(send(stats_ref.at[pl.ds(to * owned, owned)], near.at[i - 1], send_near.at[i - 1], recv_near.at[i - 1], dp, to))
    for copy in copies:
        copy.wait()
    mine[...] = merge([stats_ref[pl.ds(ex * owned, owned)]] + [near[i] for i in range(n_ex - 1)])
    copies = []
    for i in range(1, n_dp):
        copies.append(send(mine, far.at[dp], send_far.at[i - 1], recv_far.at[i - 1], lax.rem(dp + i, n_dp), ex))
    far[dp] = mine[...]
    for copy in copies:
        copy.wait()
    tiles = merge([far[i] for i in range(n_dp)])
    for copy in coming[13:]:
        copy.wait()
    blocks, wide = win.shape[1] // LANES, win.shape[2] // LANES
    for e in range(owned):
        tile = tiles[e]
        slots = tile[0:blocks] / tile[7:8]
        d_out = tile[3 : 3 + blocks]
        bias = jnp.concatenate([bin_ref[e : e + 1, LANES * j : LANES * (j + 1)] for j in range(wide)], 0)
        inner = times_columns(rows_to_columns(slots), blocks, win, e, wide) + bias
        hidden, slope = gelu_parts(inner)
        bias = jnp.concatenate([bdown_ref[e : e + 1, LANES * j : LANES * (j + 1)] for j in range(blocks)], 0)
        out = times_columns(rows_to_columns(hidden), wide, wdown, e, blocks) + bias
        d_inner = times_rows(d_out, blocks, wdown, e, wide) * slope
        d_slots = times_rows(d_inner, wide, win, e, blocks)
        along = jnp.sum(slots * d_slots, keepdims=True)
        lane = lax.broadcasted_iota(jnp.int32, (1, LANES), 1)
        last = jnp.where(lane < LANES // 2, tile[7:8], along)
        result = jnp.concatenate([out, d_slots, tile[6:7], last], 0)
        got[e] = result
        shared_ref[ex * owned + e] = result
        own_ref[e] = jnp.concatenate([slots, d_out, jnp.zeros((2, LANES), F32)], 0)
        inner_ref[e] = jnp.concatenate([hidden, d_inner], 0)
    copies = []
    for i in range(1, n_ex):
        copies.append(send(got, shared_ref.at[pl.ds(ex * owned, owned)], send_out.at[i - 1], recv_out.at[i - 1], dp, lax.rem(ex + i, n_ex)))
    keep(own_ref, own_out)
    keep(inner_ref, inner_out)
    for copy in copies:
        copy.wait()
    keep(shared_ref, shared_out)
    for copy in going:
        copy.wait()


def norm_back(grad, hat, scale, gain):
    g = grad * gain
    return scale * (g - jnp.mean(g, -1, keepdims=True) - hat * jnp.mean(g * hat, -1, keepdims=True))


def route_kernel(live_in, wout_in, g2_in, b2_in, keys_in, cot_in, resid_in, context_in, logits_in, shared_in, own_in, inner_in,
                 act_out, dresid_out, dcontext_out, gwout_out, small_ref, gwin_out, gbin_ref, gwdown_out, gbdown_ref,
                 live_ref, wout_ref, g2_ref, b2_ref, keys_ref, cot_ref, resid_ref, context_ref, logits_ref, shared_ref, own_ref,
                 inner_ref, act_ref, dresid_ref, dcontext_ref, gwout_ref, gin, gdown, loads, stores):
    length, width = resid_ref.shape
    owned = own_ref.shape[0]
    blocks = width // LANES
    wide = gin.shape[2] // LANES
    coming = load(
        (own_in, inner_in, resid_in, shared_in, logits_in, live_in, g2_in, b2_in, keys_in, cot_in, context_in, wout_in),
        (own_ref, inner_ref, resid_ref, shared_ref, logits_ref, live_ref, g2_ref, b2_ref, keys_ref, cot_ref, context_ref, wout_ref),
        loads)
    going = []

    def keep(src, dst):
        copy = pltpu.make_async_copy(src, dst, stores.at[len(going)])
        copy.start()
        going.append(copy)

    for copy in coming[:2]:
        copy.wait()
    for e in range(owned):
        slot_cols = rows_to_columns(own_ref[e])
        hidden_cols = rows_to_columns(inner_ref[e])
        for i in range(blocks):
            col = jnp.broadcast_to(slot_cols[:, i : i + 1], (LANES, LANES))
            for j in range(wide):
                gin[e, LANES * i : LANES * (i + 1), LANES * j : LANES * (j + 1)] = col * inner_ref[e, wide + j : wide + j + 1]
        keep(gin.at[e], gwin_out.at[e])
        for j in range(wide):
            col = jnp.broadcast_to(hidden_cols[:, j : j + 1], (LANES, LANES))
            for i in range(blocks):
                gdown[e, LANES * j : LANES * (j + 1), LANES * i : LANES * (i + 1)] = col * own_ref[e, 3 + i : 4 + i]
        keep(gdown.at[e], gwdown_out.at[e])
        for j in range(wide):
            gbin_ref[e : e + 1, LANES * j : LANES * (j + 1)] = inner_ref[e, wide + j : wide + j + 1]
        for i in range(blocks):
            gbdown_ref[e : e + 1, LANES * i : LANES * (i + 1)] = own_ref[e, 3 + i : 4 + i]
    for copy in coming[2:]:
        copy.wait()
    shared = shared_ref[...]
    slot_out = from_tiles(shared, 0, 3)
    d_slots = from_tiles(shared, 3, 3)
    peak = shared[:, 6, 0:1]
    total = shared[:, 7, 0:1]
    along = shared[:, 7, LANES - 1 : LANES]
    gain = as_row(g2_ref)
    cot = cot_ref[0]
    resid = resid_ref[...]
    hat2, scale2 = norm_stats(resid)
    normed2 = hat2 * gain + as_row(b2_ref)
    logits = logits_ref[...]
    dispatch = jnp.exp(jnp.where(live_ref[...] > 0, logits, NEGATIVE) - peak) / total
    comb = jnp.exp(logits - jnp.max(logits, 0, keepdims=True))
    comb = comb * (1.0 / jnp.sum(comb, 0, keepdims=True))
    d_comb = dot(slot_out, cot, 1, 1)
    d_logits = comb * (d_comb - jnp.sum(comb * d_comb, 0, keepdims=True))
    d_logits = d_logits + dispatch * (dot(d_slots, normed2, 1, 1) - along)
    d_normed2 = dot(jnp.concatenate([dispatch, d_logits], 0), jnp.concatenate([d_slots, keys_ref[...]], 0), 0, 0)
    d_resid = cot + norm_back(d_normed2, hat2, scale2, gain)
    dresid_ref[...] = d_resid
    keep(dresid_ref, dresid_out)
    context = context_ref[...]
    gwout_ref[...] = dot(context, d_resid, 1, 0)
    keep(gwout_ref, gwout_out)
    dcontext_ref[...] = dot(wout_ref[...], d_resid, 1, 1)
    keep(dcontext_ref, dcontext_out)
    small_ref[8:16] = dot(d_logits, normed2, 1, 0)
    small_ref[4:5] = jnp.sum(d_resid, 0, keepdims=True)
    small_ref[5:6] = jnp.sum(d_normed2 * hat2, 0, keepdims=True)
    small_ref[6:7] = jnp.sum(d_normed2, 0, keepdims=True)
    small_ref[7:8] = jnp.zeros((1, width), F32)
    small_ref[0:4] = jnp.zeros((4, width), F32)
    act_ref[0] = resid + dot(comb, slot_out, 0, 0)
    keep(act_ref, act_out)
    for copy in going:
        copy.wait()


def powers(n):
    return n.bit_length() - 1


def back_kernel(n_dp, n_ex, x_in, g1_in, b1_in, wqkv_in, joined_in, context_in, attn_in, dresid_in, dcontext_in, gwout_in, small_in,
                gx_ref, grads_ref, small_ref,
                x_ref, g1_ref, b1_ref, wqkv_ref, joined_ref, context_ref, attn_ref, dresid_ref, dcontext_ref, part_ref,
                smalls, djoined_ref, normed_ref, *rest):
    halvings = 4
    boxes, rest = rest[: halvings + 1], rest[halvings + 1 :]
    mine, near, far, loads, send_sem, recv_sem, send_near, recv_near, send_far, recv_far, send_all, recv_all, local = rest
    dp, ex = lax.axis_index("dp"), lax.axis_index("expert")
    all_here = greet(n_dp, n_ex, dp, ex)
    heads = [pltpu.make_async_copy(attn_in.at[h], attn_ref.at[h], loads.at[10 + h]) for h in range(HEADS)]
    coming = load(
        (gwout_in, joined_in, dcontext_in, context_in, x_in, g1_in, b1_in, wqkv_in, dresid_in, small_in),
        (part_ref.at[0], joined_ref, dcontext_ref, context_ref, x_ref, g1_ref, b1_ref, wqkv_ref, dresid_ref, smalls), loads)
    for copy in heads:
        copy.start()
    length, width = dresid_ref.shape
    rows = part_ref.shape[1]
    bits = [("expert", 0)] + [("expert", b) for b in range(1, powers(n_ex))] + [("dp", b) for b in range(powers(n_dp))]

    def bit_of(which):
        axis, b = which
        return lax.rem((ex if axis == "expert" else dp) // (1 << b), 2)

    def flip(which, weight=1):
        axis, b = which
        step = (1 - 2 * bit_of(which)) * (1 << b) * weight
        return (0, step) if axis == "expert" else (step, 0)

    first = bit_of(bits[0])
    steps = []
    for i, which in enumerate(bits):
        if i in (1, 2):
            other = bits[3 - i]
            one, two = flip(which, 1 - first), flip(other, first)
            bit = bit_of(which) * (1 - first) + bit_of(other) * first
            steps.append((bit, (one[0] + two[0], one[1] + two[1])))
        else:
            steps.append((bit_of(which), flip(which)))
    exchanges = len(bits)
    offsets = [0]
    for i in range(halvings):
        offsets.append(pl.multiple_of(offsets[-1] + steps[i][0] * (rows >> (i + 1)), 8))
    final = rows >> halvings
    rounds = exchanges + halvings

    def launch(chunk, i):
        partner = steps[i if i < exchanges else exchanges + halvings - 1 - i][1]
        to = (dp + partner[0], ex + partner[1])
        sems = (send_sem.at[chunk, i], recv_sem.at[chunk, i])
        if i < halvings:
            size = rows >> (i + 1)
            away = pl.multiple_of(offsets[i] + (1 - steps[i][0]) * size, 8)
            src, dst = part_ref.at[chunk, pl.ds(away, size)], boxes[i].at[chunk]
        elif i < exchanges:
            src, dst = part_ref.at[chunk, pl.ds(offsets[halvings], final)], boxes[halvings].at[chunk, i - halvings]
        else:
            level = exchanges + halvings - i
            size = rows >> level
            src = dst = grads_ref.at[chunk, pl.ds(offsets[level], size)]
        return send(src, dst, *sems, *to)

    flying = {}

    def advance(chunk):
        i, copy = flying.pop(chunk)
        copy.wait()
        if i < halvings:
            size = rows >> (i + 1)
            where = pl.ds(offsets[i + 1], size)
            part_ref[chunk, where] = part_ref[chunk, where] + boxes[i][chunk]
        elif i < exchanges:
            where = pl.ds(offsets[halvings], final)
            total = part_ref[chunk, where] + boxes[halvings][chunk, i - halvings]
            if i < exchanges - 1:
                part_ref[chunk, where] = total
            else:
                grads_ref[chunk, where] = total
        if i + 1 < rounds:
            flying[chunk] = (i + 1, launch(chunk, i + 1))

    def begin(chunk):
        flying[chunk] = (0, launch(chunk, 0))

    coming[0].wait()
    all_here()
    begin(0)
    for copy in coming[1:7] + coming[9:]:
        copy.wait()
    x = x_ref[0]
    hat, scale1 = norm_stats(x)
    gain = as_row(g1_ref)
    normed_ref[0:width] = (hat * gain + as_row(b1_ref)).T
    normed_ref[width:] = jnp.ones((8, length), F32)
    scale = 1.0 / math.sqrt(HEAD_DIM)
    half = length // 2
    d_normed = None
    pair = 2 * HEAD_DIM
    for h in range(HEADS):
        at = HEAD_DIM * h
        span = slice(at, at + HEAD_DIM)
        q_hi, q_lo = parts(joined_ref[at : at + HEAD_DIM])
        k_hi, k_lo = parts(joined_ref[width + at : width + at + HEAD_DIM])
        v_hi, v_lo = parts(joined_ref[2 * width + at : 2 * width + at + HEAD_DIM])
        d_context = dcontext_ref[span]
        o_hi, o_lo = parts(d_context)
        rowsum = jnp.sum(d_context * context_ref[span], 0, keepdims=True)
        values = jnp.concatenate([v_hi, v_lo, v_hi], 0).T
        d_out = jnp.concatenate([o_hi, o_hi, o_lo], 0)
        keys = jnp.concatenate([k_hi, k_lo], 0)
        queries = jnp.concatenate([q_hi, q_lo], 0)
        outs = jnp.concatenate([o_hi, o_lo], 0)
        heads[h].wait()
        d_v = d_k = None
        for b in range(2):
            part = slice(half * b, half * (b + 1))
            attn = attn_ref[h, :, part]
            d_attn = dot(values, d_out[:, part], 1, 0, None)
            d_scores = attn * (d_attn - rowsum[:, part])
            p_hi, p_lo = parts(attn)
            s_hi, s_lo = parts(d_scores)
            both = dot(keys, s_hi, 1, 0, None)
            d_q = both[:HEAD_DIM] + both[HEAD_DIM:] + dot(k_hi, s_lo, 1, 0, None)
            djoined_ref[at : at + HEAD_DIM, part] = d_q * scale
            both = dot(outs[:, part], p_hi, 1, 1, None)
            term = both[:HEAD_DIM] + both[HEAD_DIM:] + dot(o_hi[:, part], p_lo, 1, 1, None)
            d_v = term if d_v is None else d_v + term
            both = dot(queries[:, part], s_hi, 1, 1, None)
            term = both[:HEAD_DIM] + both[HEAD_DIM:] + dot(q_hi[:, part], s_lo, 1, 1, None)
            d_k = term if d_k is None else d_k + term
        djoined_ref[width + at : width + at + HEAD_DIM] = d_k
        djoined_ref[2 * width + at : 2 * width + at + HEAD_DIM] = d_v
        for chunk in sorted(flying):
            advance(chunk)
        if h % 2:
            p = h // 2
            spans = [slice(t * width + pair * p, t * width + pair * (p + 1)) for t in range(3)]
            d_part = jnp.concatenate([djoined_ref[s] for s in spans], 0)
            grad = dot(normed_ref[...], d_part, 1, 1)
            part_ref[1 + p] = grad[:width]
            begin(1 + p)
            smalls[2:3, pair * p : pair * (p + 1)] = grad[width : width + 1, :pair]
            smalls[3:4, pair * p : pair * (p + 1)] = grad[width : width + 1, 2 * pair :]
    coming[7].wait()
    d_normed = dot(djoined_ref[...], wqkv_ref[...], 0, 1)
    coming[8].wait()
    smalls[0:1] = jnp.sum(d_normed * hat, 0, keepdims=True)
    smalls[1:2] = jnp.sum(d_normed, 0, keepdims=True)
    for chunk in sorted(flying):
        advance(chunk)
    count = width // LANES
    everything = jnp.concatenate([smalls[:, LANES * i : LANES * (i + 1)] for i in range(count)], 0)
    share = mine.shape[1]
    pad = n_ex * share - everything.shape[0]
    everything = jnp.concatenate([everything, jnp.zeros((pad, LANES), F32)], 0)
    for i in range(n_ex):
        mine[i] = everything[share * i : share * (i + 1)]
    copies = []
    for i in range(1, n_ex):
        to = lax.rem(ex + i, n_ex)
        copies.append(send(mine.at[to], near.at[i - 1], send_near.at[i - 1], recv_near.at[i - 1], dp, to))
    gx_ref[0] = dresid_ref[...] + norm_back(d_normed, hat, scale1, gain)
    for copy in copies:
        copy.wait()
    local[0] = functools.reduce(jnp.add, [mine[ex]] + [near[i] for i in range(n_ex - 1)])
    copies = []
    for i in range(1, n_dp):
        copies.append(send(local.at[0], far.at[dp], send_far.at[i - 1], recv_far.at[i - 1], lax.rem(dp + i, n_dp), ex))
    far[dp] = local[0]
    for chunk in sorted(flying):
        advance(chunk)
    for copy in copies:
        copy.wait()
    total = functools.reduce(jnp.add, [far[i] for i in range(n_dp)])
    local[1] = total
    copies = []
    for i in range(1, n_ex):
        copies.append(send(local.at[1], small_ref.at[ex], send_all.at[i - 1], recv_all.at[i - 1], dp, lax.rem(ex + i, n_ex)))
    small_ref[ex] = total
    while flying:
        for chunk in sorted(flying):
            advance(chunk)
    for copy in copies:
        copy.wait()


def finish_kernel(grads_in, small_ref, gx_in, gx_out, g1_ref, b1_ref, gwqkv_out, gbqv_ref, gwout_out, gbout_ref, g2_ref, b2_ref,
                  gkeys_ref, grads_ref, gx_ref, sems):
    width = grads_in.shape[1]
    pair = 2 * HEAD_DIM
    coming = load([grads_in.at[i] for i in range(grads_in.shape[0])] + [gx_in],
                  [grads_ref.at[i] for i in range(grads_in.shape[0])] + [gx_ref], sems)
    flat = small_ref[...].reshape(-1, LANES)
    count = width // LANES
    rows = jnp.concatenate([flat[16 * i : 16 * (i + 1)] for i in range(count)], 1)
    for ref, i in ((g1_ref, 0), (b1_ref, 1), (gbout_ref, 4), (g2_ref, 5), (b2_ref, 6)):
        ref[...] = rows[i : i + 1].reshape(width)
    gbqv_ref[...] = rows[2:4]
    gkeys_ref[...] = rows[8:16]
    going = []

    def keep(src, dst):
        copy = pltpu.make_async_copy(src, dst, sems.at[len(coming) + len(going)])
        copy.start()
        going.append(copy)

    coming[0].wait()
    keep(grads_ref.at[0], gwout_out)
    for p in range(HEADS // 2):
        coming[1 + p].wait()
        for t in range(3):
            keep(grads_ref.at[1 + p, :, pl.ds(pair * t, pair)], gwqkv_out.at[:, pl.ds(t * width + pair * p, pair)])
    coming[-1].wait()
    keep(gx_ref, gx_out)
    for copy in going:
        copy.wait()


def sds(*shape):
    return jax.ShapeDtypeStruct(shape, F32)


def vm(*shape):
    return pltpu.VMEM(shape, F32)


def dma(*shape):
    return pltpu.SemaphoreType.DMA(shape)


def solution(mesh):
    n_dp, n_ex = mesh.shape["dp"], mesh.shape["expert"]

    def on_device(patches, image_ids, pad_mask, ln1_gain, ln1_bias, w_qkv, bias_qv, w_out, bias_out, ln2_gain, ln2_bias,
                  slot_keys, w_in, bias_in, w_down, bias_down, cotangent):
        _, length, width = patches.shape
        owned, _, hidden = w_in.shape
        experts = owned * n_ex
        wide = hidden // LANES
        keys_t = slot_keys.T
        like = lambda *arrays: [pltpu.VMEM(a.shape, a.dtype) for a in arrays]
        args = (patches, image_ids, pad_mask, ln1_gain, ln1_bias, w_qkv, bias_qv, w_out, bias_out, ln2_gain, ln2_bias, keys_t,
                cotangent, w_in, bias_in, w_down, bias_down)
        resid, joined, context, attn, logits, shared, own, inner = pl.pallas_call(
            functools.partial(front_kernel, n_dp, n_ex),
            out_shape=(sds(length, width), sds(3 * width, length), sds(width, length), sds(HEADS, length, length),
                       sds(experts, length), sds(experts, 8, LANES), sds(owned, 8, LANES), sds(owned, 2 * wide, LANES)),
            in_specs=[ANY] * len(args),
            out_specs=[ANY] * 8,
            scratch_shapes=like(*args) + [
                vm(length, width), vm(3 * width, length), vm(width, length), vm(HEADS, length, length), vm(experts, length),
                vm(length, length), vm(experts, 8, LANES), vm(n_ex - 1, owned, 8, LANES), vm(owned, 8, LANES),
                vm(n_dp, owned, 8, LANES), vm(owned, 8, LANES), vm(experts, 8, LANES), vm(owned, 8, LANES),
                vm(owned, 2 * wide, LANES), dma(len(args)), dma(HEADS + 7), dma(n_ex - 1), dma(n_ex - 1), dma(n_dp - 1),
                dma(n_dp - 1), dma(n_ex - 1), dma(n_ex - 1)],
            compiler_params=pltpu.CompilerParams(collective_id=0, has_side_effects=True, vmem_limit_bytes=FRONT_VMEM),
            name="front",
        )(*args)
        args = (pad_mask, w_out, ln2_gain, ln2_bias, keys_t, cotangent, resid, context, logits, shared, own, inner)
        act, d_resid, d_context, gwout, small, gwin, gbin, gwdown, gbdown = pl.pallas_call(
            route_kernel,
            out_shape=(sds(1, length, width), sds(length, width), sds(width, length), sds(width, width), sds(16, width),
                       sds(*w_in.shape), sds(*bias_in.shape), sds(*w_down.shape), sds(*bias_down.shape)),
            in_specs=[ANY] * len(args),
            out_specs=[ANY] * 4 + [VMEM, ANY, VMEM, ANY, VMEM],
            scratch_shapes=like(*args) + [vm(1, length, width), vm(length, width), vm(width, length), vm(width, width),
                                          vm(*w_in.shape), vm(*w_down.shape), dma(len(args)), dma(2 * owned + 4)],
            compiler_params=pltpu.CompilerParams(vmem_limit_bytes=ROUTE_VMEM),
            name="route",
        )(*args)
        chunks = 1 + HEADS // 2
        halvings = 4
        rounds = powers(n_dp) + powers(n_ex) + halvings
        share = 16
        args = (patches, ln1_gain, ln1_bias, w_qkv, joined, context, attn, d_resid, d_context, gwout, small)
        gx, grads, small = pl.pallas_call(
            functools.partial(back_kernel, n_dp, n_ex),
            out_shape=(sds(1, length, width), sds(chunks, width, width), sds(n_ex, share, LANES)),
            in_specs=[ANY] * len(args),
            out_specs=[VMEM] * 3,
            scratch_shapes=like(*args[:9]) + [vm(chunks, width, width), vm(16, width), vm(3 * width, length), vm(width + 8, length)]
            + [vm(chunks, width >> (i + 1), width) for i in range(halvings)]
            + [vm(chunks, rounds - 2 * halvings, width >> halvings, width), vm(n_ex, share, LANES), vm(n_ex - 1, share, LANES),
               vm(n_dp, share, LANES), dma(10 + HEADS), dma(chunks, rounds), dma(chunks, rounds), dma(n_ex - 1), dma(n_ex - 1),
               dma(n_dp - 1), dma(n_dp - 1), dma(n_ex - 1), dma(n_ex - 1), vm(2, share, LANES)],
            compiler_params=pltpu.CompilerParams(collective_id=1, has_side_effects=True, vmem_limit_bytes=BACK_VMEM),
            name="back",
        )(*args)
        gx, g1, b1, gwqkv, gbqv, gwout, gbout, g2, b2, gkeys = pl.pallas_call(
            finish_kernel,
            out_shape=(sds(1, length, width), sds(width), sds(width), sds(*w_qkv.shape), sds(*bias_qv.shape), sds(*w_out.shape),
                       sds(width), sds(width), sds(width), sds(experts, width)),
            in_specs=[ANY, VMEM, ANY],
            out_specs=[ANY, VMEM, VMEM, ANY, VMEM, ANY, VMEM, VMEM, VMEM, VMEM],
            scratch_shapes=[vm(chunks, width, width), vm(1, length, width), dma(2 * chunks + 2 + 3 * chunks)],
            compiler_params=pltpu.CompilerParams(vmem_limit_bytes=FINISH_VMEM),
            name="finish",
        )(grads, small, gx)
        return (act, gx, g1, b1, gwqkv, gbqv, gwout, gbout, g2, b2, gkeys.T, gwin, gbin, gwdown, gbdown)

    rows = P(("dp", "expert"), None, None)
    flags = P(("dp", "expert"), None)
    e3, e2 = P("expert", None, None), P("expert", None)
    return jax.shard_map(
        on_device,
        mesh=mesh,
        in_specs=(rows, flags, flags) + (P(),) * 9 + (e3, e2, e3, e2, rows),
        out_specs=(rows, rows) + (P(),) * 9 + (e3, e2, e3, e2),
        check_vma=False,
    )
```

time: 231 us -> 108 us (0.47)
  waiting for transfers between devices: 93.3 us -> 0 us
  Pallas kernels: 51.5 us -> 103 us
  blocking collectives: 40.2 us -> 0 us
  local copies, waits for them, and re-layouts: 31 us -> 3.55 us
  between operations: 14.2 us -> 0.86 us
    psum x1 -> x0, waiting for transfers between devices: 93.3 us -> none  [on_device(): gwqkv, gwout, small = lax.psum((gwqkv, gwout, small), ('dp', 'expert'))]
    pallas_call x3 -> x4, Pallas kernels: 51.5 us -> 103 us  [the longest x1 62.9 us: on_device(): pl.pallas_call(functools.partial(back_kernel, n_dp, n_ex), out_shape=(sds...]
    psum x1 -> x0, blocking collectives: 40.2 us -> none  [on_device(): gwqkv, gwout, small = lax.psum((gwqkv, gwout, small), ('dp', 'expert'))]
    unnamed x59 -> x6, local copies, waits for them, and re-layouts: 25.7 us -> 3.55 us
    reshape x5 -> x0, local copies, waits for them, and re-layouts: 3.45 us -> none  [on_device(): row = lambda v: v.reshape(1, -1)]
  transfers between devices with their start and end apart: 1 -> 0, of which waited for: 1 -> 0; matrix products, arithmetic and copies ran while one was open for 1% -> 0% of each run, Pallas kernels for 0% -> 0%
where the time goes in v1:
time: 108 us; the launch traced here: 107 us
  Pallas kernels  103 us (95%)
  local copies, waits for them, and re-layouts  3.55 us (3%)
    pallas_call x1, Pallas kernels, on_device(): pl.pallas_call(functools.partial(back_kernel, n_dp, n_ex), out_shape=(sds...  62.9 us
    pallas_call x1, Pallas kernels, on_device(): pl.pallas_call(functools.partial(front_kernel, n_dp, n_ex), out_shape=(sd...  29.8 us
    pallas_call x1, Pallas kernels, on_device(): pl.pallas_call(route_kernel, out_shape=(sds(1, length, width), sds(length...  7.23 us
    unnamed x6, local copies, waits for them, and re-layouts  3.55 us
    pallas_call x1, Pallas kernels, on_device(): pl.pallas_call(finish_kernel, out_shape=(sds(1, length, width), sds(width...  3.01 us

profile of v1, /device:TPU:0, one launch (start us, length us, event | category | flops | bytes accessed | tf_op | source)
XLA Modules:
  0.0 107.3 jit_solution(5188083556617278513)
XLA Ops:
  0.6 29.8 %front.1 = (f32[512,384]{1,0:T(8,128)}, f32[1152,512]{1,0:T(8,128)}, f32[384,512]{1,0:T(8,128)}, f32[6,512,512]{2,1,0:T(8,128)}, f32[8,512]{1,0:T(8,128)}, /*ind...) custom-call(f32[1,512,384]{2,1,0:T(8,128)} %x_in.3, s32[1,512]{1,0:T(1,128)} %ids_in.1, ...), custom_call_target="tpu_custom_call" | custom-call | tf_op jit(solution)/shard_map/front/pallas_call | solution.py:594
  30.5 7.2 %route.1 = (f32[1,512,384]{2,1,0:T(8,128)}, f32[512,384]{1,0:T(8,128)}, f32[384,512]{1,0:T(8,128)}, f32[384,384]{1,0:T(8,128)}, f32[16,384]{1,0:T(8,128)}, /*ind...) custom-call(s32[1,512]{1,0:T(1,128)} %live_in.3, f32[384,384]{1,0:T(8,128)} %wout_in.3, ...), custom_call_target="tpu_custom_call" | custom-call | tf_op jit(solution)/shard_map/route/pallas_call | solution.py:610
  37.7 62.9 %back.1 = (f32[1,512,384]{2,1,0:T(8,128)}, f32[4,384,384]{2,1,0:T(8,128)}, f32[4,16,128]{2,1,0:T(8,128)}) custom-call(f32[1,512,384]{2,1,0:T(8,128)} %x_in.3, f32[384]{0:T(512)} %g1_in.3, f32[384]{0:T(512)} %b1_in.3, f32[384,1152]{1,0:T(8,128)} %wqkv_in.3, f32[1152,512]{1,0:T(8,128)} %get-tuple-element.52.joined_in, ...), custom_call_target="tpu_custom_call" | custom-call | tf_op jit(solution)/shard_map/back/pallas_call | solution.py:626
  100.6 0.0 copy-start
  100.6 1.7 %copy-done = f32[4,384,384]{2,1,0:T(8,128)S(1)} copy-done((f32[4,384,384]{2,1,0:T(8,128)S(1)}, f32[4,384,384]{2,1,0:T(8,128)}, u32[]{:S(2)}) %copy-start) | copy-done | bytes 2359320
  102.2 0.0 copy-start.1
  102.2 1.1 %copy-done.1 = f32[1,512,384]{2,1,0:T(8,128)S(1)} copy-done((f32[1,512,384]{2,1,0:T(8,128)S(1)}, f32[1,512,384]{2,1,0:T(8,128)}, u32[]{:S(2)}) %copy-start.1) | copy-done | bytes 786456
  103.4 0.0 copy-start.2
  103.4 0.8 copy-done.2
  104.1 3.0 %finish.1 = (f32[1,512,384]{2,1,0:T(8,128)}, f32[384]{0:T(512)}, f32[384]{0:T(512)}, f32[384,1152]{1,0:T(8,128)}, f32[2,384]{1,0:T(2,128)}, /*index=5*/f32[384,3...) custom-call(f32[4,384,384]{2,1,0:T(8,128)S(1)} %copy-done, f32[4,16,128]{2,1,0:T(8,128)S(1)} %copy-done.2, ...), custom_call_target="tpu_custom_call" | custom-call | tf_op jit(solution)/shard_map/finish/pallas_call | solution.py:639
Async XLA Ops:
  100.6 1.7 %copy-start = (f32[4,384,384]{2,1,0:T(8,128)S(1)}, f32[4,384,384]{2,1,0:T(8,128)}, u32[]{:S(2)}) copy-start(f32[4,384,384]{2,1,0:T(8,128)} %get-tuple-element.58.grads_in) | copy-start | bytes 7077892
  102.2 1.1 %copy-start.1 = (f32[1,512,384]{2,1,0:T(8,128)S(1)}, f32[1,512,384]{2,1,0:T(8,128)}, u32[]{:S(2)}) copy-start(f32[1,512,384]{2,1,0:T(8,128)} %get-tuple-element.60.gx_in) | copy-start | bytes 2359300
  103.4 0.8 copy-start.2

commit v2 on v0

v2 whole, which is shorter than its diff:
```python
import functools
import math

import jax
import jax.numpy as jnp
from jax import lax
from jax.experimental import pallas as pl
from jax.experimental.pallas import tpu as pltpu
from jax.sharding import PartitionSpec as P

HEADS = 6
HEAD_DIM = 64
LANES = 128
EPSILON = 1e-06
NEGATIVE = -1e30
HIGH = lax.Precision.HIGH
BF = jnp.bfloat16
F32 = jnp.float32
MESH = pl.DeviceIdType.MESH
LAYER_VMEM = 56 << 20
FINISH_VMEM = 56 << 20
PLAN = {
    "kinds": ('direct', 'direct', 'direct', 'direct', 'direct', 'direct', 'small'),
    "ticks": {3: (0,), 10: (1,), 12: (0,), 13: (2,), 17: (3,), 18: (1,), 19: (4, 2), 20: (5,)},
    "drain": (0, 3, 6, 4, 5, 1, 0, 0, 2, 1, 3, 1, 6, 2, 4, 2, 5, 6, 3, 3, 4, 4, 5, 5),
}
VMEM = pl.BlockSpec(memory_space=pltpu.VMEM)
ANY = pl.BlockSpec(memory_space=pl.ANY)


def dot(left, right, dim_left, dim_right, precision=HIGH):
    return lax.dot_general(
        left, right, (((dim_left,), (dim_right,)), ((), ())), precision=precision, preferred_element_type=F32
    )


def parts(value):
    high = value.astype(BF)
    return high, (value - high.astype(F32)).astype(BF)


def norm_stats(values):
    center = values - jnp.mean(values, -1, keepdims=True)
    spread = jnp.mean(center * center, -1, keepdims=True)
    scale = lax.rsqrt(spread + EPSILON)
    return center * scale, scale


def column(row):
    return jnp.broadcast_to(row, (8, row.shape[1])).T[:, :1]


def load(sources, targets, sems):
    copies = [pltpu.make_async_copy(src, dst, sems.at[i]) for i, (src, dst) in enumerate(zip(sources, targets))]
    for copy in copies:
        copy.start()
    return copies


def greet(n_dp, n_ex, dp, ex):
    barrier = pltpu.get_barrier_semaphore()
    for i in range(1, n_ex):
        pl.semaphore_signal(barrier, inc=1, device_id=(dp, lax.rem(ex + i, n_ex)), device_id_type=MESH)
    for i in range(1, n_dp):
        pl.semaphore_signal(barrier, inc=1, device_id=(lax.rem(dp + i, n_dp), ex), device_id_type=MESH)
    return lambda: pl.semaphore_wait(barrier, n_ex + n_dp - 2)


def send(src, dst, out_sem, in_sem, dp, ex):
    copy = pltpu.make_async_remote_copy(
        src_ref=src, dst_ref=dst, send_sem=out_sem, recv_sem=in_sem, device_id=(dp, ex), device_id_type=MESH)
    copy.start()
    return copy


def as_row(ref):
    return ref[...].reshape(1, -1)


def to_tiles(rows):
    return jnp.stack([jnp.concatenate([rows[e : e + 1, LANES * i : LANES * (i + 1)] for i in range(8)], 0) for e in range(rows.shape[0])], 0)


def from_tiles(tiles, first, count):
    return jnp.concatenate([tiles[:, first + i, :] for i in range(count)], -1)


def merge(tiles):
    peaks = [tile[:, 6:7, :] for tile in tiles]
    peak = functools.reduce(jnp.maximum, peaks)
    row = lax.broadcasted_iota(jnp.int32, tiles[0].shape, 1)
    weighted = (row < 3) | (row == 7)
    total = None
    for tile, own in zip(tiles, peaks):
        scaled = jnp.where(weighted, tile * jnp.exp(own - peak), tile)
        total = scaled if total is None else total + scaled
    return jnp.where(row == 6, peak, total)


def gelu_parts(inner):
    phi = 0.5 * (1.0 + lax.erf(inner * (1.0 / math.sqrt(2.0))))
    density = jnp.exp(-0.5 * inner * inner) * (1.0 / math.sqrt(2.0 * math.pi))
    return inner * phi, phi + inner * density


def rows_to_columns(rows):
    pad = -rows.shape[0] % 8
    if pad:
        rows = jnp.concatenate([rows, jnp.zeros((pad, LANES), F32)], 0)
    return rows.T


def times_columns(cols, count, w_ref, e, lanes):
    wide = [jnp.broadcast_to(cols[:, i : i + 1], (LANES, LANES)) for i in range(count)]
    rows = []
    for j in range(lanes):
        acc = None
        for i in range(count):
            term = wide[i] * w_ref[e, LANES * i : LANES * (i + 1), LANES * j : LANES * (j + 1)]
            term = jnp.sum(term.reshape(LANES // 8, 8, LANES), 0)
            acc = term if acc is None else acc + term
        rows.append(jnp.sum(acc, 0, keepdims=True))
    return jnp.concatenate(rows, 0)


def times_rows(rows, count, w_ref, e, blocks):
    out = []
    for i in range(blocks):
        acc = None
        for j in range(count):
            term = rows[j : j + 1] * w_ref[e, LANES * i : LANES * (i + 1), LANES * j : LANES * (j + 1)]
            acc = term if acc is None else acc + term
        out.append(jnp.sum(acc.T, 0, keepdims=True))
    return jnp.concatenate(out, 0)


def norm_back(grad, hat, scale, gain):
    g = grad * gain
    return scale * (g - jnp.mean(g, -1, keepdims=True) - hat * jnp.mean(g * hat, -1, keepdims=True))


def powers(n):
    return n.bit_length() - 1


HALVINGS = 4
INPUTS = ("x", "g1", "b1", "wqkv", "bqv", "ids", "wout", "bout", "g2", "b2", "keys", "live", "cot", "win", "bin", "wdown", "bdown")


def layer_kernel(n_dp, n_ex, names, *refs):
    at = dict(zip(names, refs))
    dp, ex = lax.axis_index("dp"), lax.axis_index("expert")
    stats_ref, near, mine, far, got, shared_ref, own_ref, inner_ref = (
        at[n] for n in ("stats", "near", "mine", "far", "got", "shared", "own", "inner"))
    win, wdown, bin_ref, bdown_ref = at["win"], at["wdown"], at["bin"], at["bdown"]
    joined_ref, context_ref, attn_ref, block_ref = at["joined"], at["context"], at["attn"], at["block"]
    high_ref, low_ref, kk_ref, qq_ref, vt_ref = at["high"], at["low"], at["kk"], at["qq"], at["vt"]
    djoined_ref, normed_ref, smalls = at["djoined"], at["normed"], at["smalls"]
    sems = at["sems"]
    owned = win.shape[0]
    all_here = greet(n_dp, n_ex, dp, ex)
    coming = dict(zip(INPUTS, load([at[n + "_in"] for n in INPUTS], [at[n] for n in INPUTS], at["loads"])))

    def ready(*which):
        for n in which:
            coming[n].wait()

    ready("x", "g1", "b1")
    x = at["x"][0]
    length, width = x.shape
    half = length // 2
    halves = [slice(half * b, half * (b + 1)) for b in range(2)]
    hat, _ = norm_stats(x)
    normed = hat * as_row(at["g1"]) + as_row(at["b1"])
    ready("wqkv", "bqv", "ids")
    joined = dot(at["wqkv"][...], normed, 0, 1)
    bias = jnp.broadcast_to(at["bqv"][0:1], (8, width)).T[:, :1]
    bias_v = jnp.broadcast_to(at["bqv"][1:2], (8, width)).T[:, :1]
    scale = 1.0 / math.sqrt(HEAD_DIM)
    joined_ref[0:width] = (joined[:width] + bias) * scale
    joined_ref[width : 2 * width] = joined[width : 2 * width]
    joined_ref[2 * width :] = joined[2 * width :] + bias_v
    ids = at["ids"][...].astype(F32)
    block_ref[...] = jnp.where(column(ids) == ids, 0.0, NEGATIVE)
    for h in range(HEADS):
        lo = HEAD_DIM * h
        q_hi, q_lo = parts(joined_ref[lo : lo + HEAD_DIM])
        k_hi, k_lo = parts(joined_ref[width + lo : width + lo + HEAD_DIM])
        v_hi, v_lo = parts(joined_ref[2 * width + lo : 2 * width + lo + HEAD_DIM])
        queries = jnp.concatenate([q_hi, q_hi, q_lo], 0)
        keys = jnp.concatenate([k_hi, k_lo, k_hi], 0).T
        values = jnp.concatenate([v_hi, v_lo], 0)
        kk_ref[h] = jnp.concatenate([k_hi, k_lo], 0)
        qq_ref[h] = jnp.concatenate([q_hi, q_lo], 0)
        vt_ref[h] = values
        for part in halves:
            scores = dot(keys, queries[:, part], 1, 0, None) + block_ref[:, part]
            expo = jnp.exp(scores - jnp.max(scores, 0, keepdims=True))
            attn = expo * (1.0 / jnp.sum(expo, 0, keepdims=True))
            attn_ref[h, :, part] = attn
            p_hi, p_lo = parts(attn)
            high_ref[h, :, part] = p_hi
            low_ref[h, :, part] = p_lo
            both = dot(values, p_hi, 1, 0, None)
            context_ref[lo : lo + HEAD_DIM, part] = both[:HEAD_DIM] + both[HEAD_DIM:] + dot(v_hi, p_lo, 1, 0, None)
    ready("wout", "bout", "g2", "b2", "keys", "live", "cot")
    context = context_ref[...]
    resid = x + dot(context, at["wout"][...], 0, 0) + as_row(at["bout"])
    gain2 = as_row(at["g2"])
    hat2, scale2 = norm_stats(resid)
    normed2 = hat2 * gain2 + as_row(at["b2"])
    logits = dot(at["keys"][...], normed2, 1, 1)
    masked = jnp.where(at["live"][...] > 0, logits, NEGATIVE)
    peak = jnp.max(masked, 1, keepdims=True)
    expo = jnp.exp(masked - peak)
    total = jnp.sum(expo, 1, keepdims=True)
    summed = dot(expo, normed2, 1, 0)
    comb = jnp.exp(logits - jnp.max(logits, 0, keepdims=True))
    comb = comb * (1.0 / jnp.sum(comb, 0, keepdims=True))
    cot = at["cot"][0]
    part_out = dot(comb, cot, 1, 0)
    experts = logits.shape[0]
    stats_ref[...] = to_tiles(jnp.concatenate(
        [summed, part_out, jnp.broadcast_to(peak, (experts, LANES)), jnp.broadcast_to(total, (experts, LANES))], 1))
    all_here()
    copies = []
    for i in range(1, n_ex):
        to = lax.rem(ex + i, n_ex)
        copies.append(send(stats_ref.at[pl.ds(to * owned, owned)], near.at[i - 1], sems.at[0, 0, i], sems.at[1, 0, i], dp, to))
    normed_ref[0:width] = normed.T
    normed_ref[width:] = jnp.ones((8, length), F32)
    for copy in copies:
        copy.wait()
    mine[...] = merge([stats_ref[pl.ds(ex * owned, owned)]] + [near[i] for i in range(n_ex - 1)])
    copies = []
    for i in range(1, n_dp):
        copies.append(send(mine, far.at[dp], sems.at[0, 1, i], sems.at[1, 1, i], lax.rem(dp + i, n_dp), ex))
    far[dp] = mine[...]
    ready("win", "bin", "wdown", "bdown")
    for copy in copies:
        copy.wait()
    tiles = merge([far[i] for i in range(n_dp)])
    blocks, wide = win.shape[1] // LANES, win.shape[2] // LANES
    for e in range(owned):
        tile = tiles[e]
        slots = tile[0:blocks] / tile[7:8]
        d_out = tile[3 : 3 + blocks]
        bias = jnp.concatenate([bin_ref[e : e + 1, LANES * j : LANES * (j + 1)] for j in range(wide)], 0)
        inner = times_columns(rows_to_columns(slots), blocks, win, e, wide) + bias
        hidden, slope = gelu_parts(inner)
        bias = jnp.concatenate([bdown_ref[e : e + 1, LANES * j : LANES * (j + 1)] for j in range(blocks)], 0)
        out = times_columns(rows_to_columns(hidden), wide, wdown, e, blocks) + bias
        d_inner = times_rows(d_out, blocks, wdown, e, wide) * slope
        d_slots = times_rows(d_inner, wide, win, e, blocks)
        along = jnp.sum(slots * d_slots, keepdims=True)
        lane = lax.broadcasted_iota(jnp.int32, (1, LANES), 1)
        last = jnp.where(lane < LANES // 2, tile[7:8], along)
        result = jnp.concatenate([out, d_slots, tile[6:7], last], 0)
        got[e] = result
        shared_ref[ex * owned + e] = result
        own_ref[e] = jnp.concatenate([slots, d_out, jnp.zeros((2, LANES), F32)], 0)
        inner_ref[e] = jnp.concatenate([hidden, d_inner], 0)
    copies = []
    for i in range(1, n_ex):
        copies.append(send(got, shared_ref.at[pl.ds(ex * owned, owned)], sems.at[0, 2, i], sems.at[1, 2, i], dp, lax.rem(ex + i, n_ex)))
    for copy in copies:
        copy.wait()

    bits = [("expert", 0)] + [("expert", b) for b in range(1, powers(n_ex))] + [("dp", b) for b in range(powers(n_dp))]

    def bit_of(which):
        axis, b = which
        return lax.rem((ex if axis == "expert" else dp) // (1 << b), 2)

    def flip(which, weight=1):
        axis, b = which
        step = (1 - 2 * bit_of(which)) * (1 << b) * weight
        return (0, step) if axis == "expert" else (step, 0)

    first = bit_of(bits[0])
    steps = []
    for i, which in enumerate(bits):
        if i in (1, 2):
            other = bits[3 - i]
            one, two = flip(which, 1 - first), flip(other, first)
            bit = bit_of(which) * (1 - first) + bit_of(other) * first
            steps.append((bit, (one[0] + two[0], one[1] + two[1])))
        else:
            steps.append((bit_of(which), flip(which)))
    exchanges = len(bits)

    def halving(chunk):
        part, total, *boxes, send_sem, recv_sem = chunk
        rows = part.shape[0]
        offsets = [0]
        for i in range(HALVINGS):
            offsets.append(pl.multiple_of(offsets[-1] + steps[i][0] * (rows >> (i + 1)), 8))
        final = pl.ds(offsets[HALVINGS], rows >> HALVINGS)

        def start(i):
            partner = steps[i if i < exchanges else exchanges + HALVINGS - 1 - i][1]
            if i < HALVINGS:
                size = rows >> (i + 1)
                away = pl.multiple_of(offsets[i] + (1 - steps[i][0]) * size, 8)
                src, dst = part.at[pl.ds(away, size)], boxes[i]
            elif i < exchanges:
                src, dst = part.at[final], boxes[HALVINGS].at[i - HALVINGS]
            else:
                level = exchanges + HALVINGS - i
                src = dst = total.at[pl.ds(offsets[level], rows >> level)]
            return [send(src, dst, send_sem.at[i], recv_sem.at[i], dp + partner[0], ex + partner[1])]

        def absorb(i):
            if i < HALVINGS:
                where = pl.ds(offsets[i + 1], rows >> (i + 1))
                part[where] = part[where] + boxes[i][...]
            elif i < exchanges - 1:
                part[final] = part[final] + boxes[HALVINGS][i - HALVINGS]
            elif i == exchanges - 1:
                total[final] = part[final] + boxes[HALVINGS][i - HALVINGS]

        return start, absorb, exchanges + HALVINGS

    x_bit, y_bit = bit_of(("expert", 1)), bit_of(("dp", 0))
    deep, n_deep = dp // 2, n_dp // 2

    def direct(chunk):
        part, total, box_core, box_plane, box_deep, wires = chunk
        rows = part.shape[0]
        half, quarter = rows // 2, rows // 8
        base = pl.multiple_of(first * half, 8)
        away = pl.multiple_of((1 - first) * half, 8)

        def spot(j):
            flip_x, flip_y = j % 2, j // 2
            to_x = x_bit + (1 - 2 * x_bit) * flip_x
            to_y = y_bit + (1 - 2 * y_bit) * flip_y
            row = pl.multiple_of(base + quarter * (to_x + 2 * to_y), 8)
            return pl.ds(row, quarter), dp + (to_y - y_bit), ex + 2 * (to_x - x_bit)

        own = spot(0)[0]

        def start(i):
            if i in (0, 4):
                core = (dp, ex + 1 - 2 * first)
                src, dst = (part.at[pl.ds(away, half)], box_core) if i == 0 else (total.at[pl.ds(base, half)],) * 2
                return [send(src, dst, wires.at[0, i], wires.at[1, i], *core)]
            copies = []
            if i == 2:
                for k in range(1, n_deep):
                    copies.append(send(part.at[own], box_deep.at[deep], wires.at[0, 10 + k], wires.at[1, 10 + k], lax.rem(dp + 2 * k, n_dp), ex))
                box_deep[deep] = part[own]
            else:
                for j in range(1, 4):
                    where, to_dp, to_ex = spot(j)
                    src, dst = (part.at[where], box_plane.at[j - 1]) if i == 1 else (total.at[own],) * 2
                    at = (4 if i == 1 else 7) + j
                    copies.append(send(src, dst, wires.at[0, at], wires.at[1, at], to_dp, to_ex))
            return copies

        def absorb(i):
            if i == 0:
                part[pl.ds(base, half)] = part[pl.ds(base, half)] + box_core[...]
            elif i == 1:
                part[own] = (part[own] + box_plane[0]) + (box_plane[1] + box_plane[2])
            elif i == 2:
                total[own] = functools.reduce(jnp.add, [box_deep[k] for k in range(n_deep)])

        return start, absorb, 5

    def small(chunk):
        to_near, from_near, from_far, local, result = chunk

        def start(i):
            copies = []
            if i == 1:
                for k in range(1, n_dp):
                    copies.append(send(local.at[0], from_far.at[dp], sems.at[0, 4, k], sems.at[1, 4, k], lax.rem(dp + k, n_dp), ex))
                from_far[dp] = local[0]
                return copies
            for k in range(1, n_ex):
                to = lax.rem(ex + k, n_ex)
                src, dst = (to_near.at[to], from_near.at[k - 1]) if i == 0 else (local.at[1], result.at[ex])
                copies.append(send(src, dst, sems.at[0, 3 + i, k], sems.at[1, 3 + i, k], dp, to))
            if i == 2:
                result[ex] = local[1]
            return copies

        def absorb(i):
            if i == 0:
                local[0] = functools.reduce(jnp.add, [to_near[ex]] + [from_near[k] for k in range(n_ex - 1)])
            elif i == 1:
                local[1] = functools.reduce(jnp.add, [from_far[k] for k in range(n_dp)])

        return start, absorb, 3

    kinds = {"halving": halving, "direct": direct, "small": small}
    chunks = [[at[f"c{c}_{i}"] for i in range(sum(n.startswith(f"c{c}_") for n in names))] for c in range(len(PLAN["kinds"]))]
    flying = {}
    slot = [0]

    def begin(c):
        start, absorb, rounds = kinds[PLAN["kinds"][c]](chunks[c])
        flying[c] = [start, absorb, rounds, 0, start(0)]

    def advance(c):
        if c not in flying:
            return
        start, absorb, rounds, i, copies = flying[c]
        for copy in copies:
            copy.wait()
        absorb(i)
        if i + 1 < rounds:
            flying[c][3:] = [i + 1, start(i + 1)]
        else:
            del flying[c]

    def tick():
        for c in PLAN["ticks"].get(slot[0], ()):
            advance(c)
        slot[0] += 1

    shared = shared_ref[...]
    slot_out = from_tiles(shared, 0, 3)
    d_slots = from_tiles(shared, 3, 3)
    peak = shared[:, 6, 0:1]
    total = shared[:, 7, 0:1]
    along = shared[:, 7, LANES - 1 : LANES]
    dispatch = jnp.exp(masked - peak) / total
    d_comb = dot(slot_out, cot, 1, 1)
    d_logits = comb * (d_comb - jnp.sum(comb * d_comb, 0, keepdims=True))
    d_logits = d_logits + dispatch * (dot(d_slots, normed2, 1, 1) - along)
    d_normed2 = dot(jnp.concatenate([dispatch, d_logits], 0), jnp.concatenate([d_slots, at["keys"][...]], 0), 0, 0)
    d_resid = cot + norm_back(d_normed2, hat2, scale2, gain2)
    chunks[0][0][...] = dot(context_ref[...], d_resid, 1, 0)
    begin(0)
    d_context = dot(at["wout"][...], d_resid, 1, 1)
    tick()
    outs = []
    for h in range(HEADS):
        lo = HEAD_DIM * h
        o_hi, o_lo = parts(d_context[lo : lo + HEAD_DIM])
        outs.append((o_hi, o_lo))
        both = jnp.concatenate([o_hi, o_lo], 0)
        d_v = None
        for part in halves:
            high = dot(both[:, part], high_ref[h, :, part], 1, 1, None)
            term = high[:HEAD_DIM] + high[HEAD_DIM:] + dot(o_hi[:, part], low_ref[h, :, part], 1, 1, None)
            d_v = term if d_v is None else d_v + term
        djoined_ref[2 * width + lo : 2 * width + lo + HEAD_DIM] = d_v
        tick()
    grad = dot(normed_ref[...], djoined_ref[2 * width :], 1, 1)
    chunks[1][0][...] = grad[:width]
    begin(1)
    smalls[3:4] = grad[width : width + 1]
    launch_at = {1: (2, 0, 2), 3: (3, 2, 4), 4: (4, 4, 5), 5: (5, 5, 6)}
    for h in range(HEADS):
        lo = HEAD_DIM * h
        span = slice(lo, lo + HEAD_DIM)
        o_hi, o_lo = outs[h]
        rowsum = jnp.sum(d_context[span] * context_ref[span], 0, keepdims=True)
        v_both, keys, queries = vt_ref[h], kk_ref[h], qq_ref[h]
        values = jnp.concatenate([v_both, v_both[:HEAD_DIM]], 0).T
        d_out = jnp.concatenate([o_hi, o_hi, o_lo], 0)
        d_k = None
        for part in halves:
            d_attn = dot(values, d_out[:, part], 1, 0, None)
            s_hi, s_lo = parts(attn_ref[h, :, part] * (d_attn - rowsum[:, part]))
            both = dot(keys, s_hi, 1, 0, None)
            d_q = both[:HEAD_DIM] + both[HEAD_DIM:] + dot(keys[:HEAD_DIM], s_lo, 1, 0, None)
            djoined_ref[span, part] = d_q * scale
            both = dot(queries[:, part], s_hi, 1, 1, None)
            term = both[:HEAD_DIM] + both[HEAD_DIM:] + dot(queries[:HEAD_DIM, part], s_lo, 1, 1, None)
            d_k = term if d_k is None else d_k + term
            tick()
        djoined_ref[width + lo : width + lo + HEAD_DIM] = d_k
        if h in launch_at:
            c, lo, hi = launch_at[h]
            lo, hi = lo * HEAD_DIM, hi * HEAD_DIM
            d_part = jnp.concatenate([djoined_ref[lo:hi], djoined_ref[width + lo : width + hi]], 0)
            grad = dot(normed_ref[...], d_part, 1, 1)
            chunks[c][0][...] = grad[:width]
            begin(c)
            row = grad[width : width + 1, : hi - lo]
            if (hi - lo) % LANES == 0:
                smalls[2:3, lo:hi] = row
            elif lo % LANES == 0:
                kept_row = row
            else:
                smalls[2:3, lo - HEAD_DIM : hi] = jnp.concatenate([kept_row, row], 1)
    d_normed = dot(djoined_ref[...], at["wqkv"][...], 0, 1)
    tick()
    hat, scale1 = norm_stats(x)
    smalls[0:1] = jnp.sum(d_normed * hat, 0, keepdims=True)
    smalls[1:2] = jnp.sum(d_normed, 0, keepdims=True)
    smalls[4:5] = jnp.sum(d_resid, 0, keepdims=True)
    smalls[5:6] = jnp.sum(d_normed2 * hat2, 0, keepdims=True)
    smalls[6:7] = jnp.sum(d_normed2, 0, keepdims=True)
    smalls[7:8] = jnp.zeros((1, width), F32)
    smalls[8:16] = dot(d_logits, normed2, 1, 0)
    count = width // LANES
    everything = jnp.concatenate([smalls[:, LANES * i : LANES * (i + 1)] for i in range(count)], 0)
    to_near = chunks[6][0]
    share = to_near.shape[1]
    everything = jnp.concatenate([everything, jnp.zeros((n_ex * share - everything.shape[0], LANES), F32)], 0)
    for i in range(n_ex):
        to_near[i] = everything[share * i : share * (i + 1)]
    begin(6)
    tick()
    at["gx_out"][0] = d_resid + norm_back(d_normed, hat, scale1, as_row(at["g1"]))
    tick()
    at["act_out"][0] = resid + dot(comb, slot_out, 0, 0)
    tick()
    for c in PLAN["drain"]:
        advance(c)
    while flying:
        for c in sorted(flying):
            advance(c)


FINISH = ("own", "inner", "small", "act", "gx", "gwout", "gv", "gqk0", "gqk1", "gqk2", "gqk3")


def finish_kernel(*refs):
    n = len(FINISH)
    sources, results, (gin, gdown, gqk_ref, *boxes, loads, stores) = refs[:n], refs[n : n + 15], refs[n + 15 :]
    (act_out, gx_out, g1_ref, b1_ref, gwqkv_out, gbqv_ref, gwout_out, gbout_ref, g2_ref, b2_ref, gkeys_ref,
     gwin_out, gbin_ref, gwdown_out, gbdown_ref) = results
    at = dict(zip(FINISH, boxes))
    coming = dict(zip(FINISH, load(sources, boxes, loads)))
    own_ref, inner_ref, small_ref = at["own"], at["inner"], at["small"]
    width = at["gv"].shape[1]
    owned = own_ref.shape[0]
    blocks, wide = width // LANES, gin.shape[2] // LANES
    pair = 2 * HEAD_DIM
    going = []

    def keep(src, dst):
        copy = pltpu.make_async_copy(src, dst, stores.at[len(going)])
        copy.start()
        going.append(copy)

    for name in ("own", "inner"):
        coming[name].wait()
    for e in range(owned):
        slot_cols = rows_to_columns(own_ref[e])
        hidden_cols = rows_to_columns(inner_ref[e])
        for i in range(blocks):
            col = jnp.broadcast_to(slot_cols[:, i : i + 1], (LANES, LANES))
            for j in range(wide):
                gin[e, LANES * i : LANES * (i + 1), LANES * j : LANES * (j + 1)] = col * inner_ref[e, wide + j : wide + j + 1]
            keep(gin.at[e, pl.ds(LANES * i, LANES)], gwin_out.at[e, pl.ds(LANES * i, LANES)])
        third = wide // 3
        for j in range(wide):
            col = jnp.broadcast_to(hidden_cols[:, j : j + 1], (LANES, LANES))
            for i in range(blocks):
                gdown[e, LANES * j : LANES * (j + 1), LANES * i : LANES * (i + 1)] = col * own_ref[e, 3 + i : 4 + i]
            if (j + 1) % third == 0:
                rows = pl.ds(LANES * (j + 1 - third), LANES * third)
                keep(gdown.at[e, rows], gwdown_out.at[e, rows])
        for j in range(wide):
            gbin_ref[e : e + 1, LANES * j : LANES * (j + 1)] = inner_ref[e, wide + j : wide + j + 1]
        for i in range(blocks):
            gbdown_ref[e : e + 1, LANES * i : LANES * (i + 1)] = own_ref[e, 3 + i : 4 + i]
    for name, out in (("act", act_out), ("gx", gx_out), ("gwout", gwout_out), ("gv", gwqkv_out.at[:, pl.ds(2 * width, width)])):
        coming[name].wait()
        keep(at[name], out)
    for p in range(2):
        coming[f"gqk{p}"].wait()
        for t in range(2):
            keep(at[f"gqk{p}"].at[:, pl.ds(pair * t, pair)], gwqkv_out.at[:, pl.ds(t * width + pair * p, pair)])
    for name in ("gqk2", "gqk3", "small"):
        coming[name].wait()
    one, two = at["gqk2"][...], at["gqk3"][...]
    gqk_ref[0] = jnp.concatenate([one[:, :HEAD_DIM], two[:, :HEAD_DIM]], 1)
    gqk_ref[1] = jnp.concatenate([one[:, HEAD_DIM:], two[:, HEAD_DIM:]], 1)
    for t in range(2):
        keep(gqk_ref.at[t], gwqkv_out.at[:, pl.ds(t * width + 2 * pair, pair)])
    flat = small_ref[...].reshape(-1, LANES)
    rows = jnp.concatenate([flat[16 * i : 16 * (i + 1)] for i in range(blocks)], 1)
    for ref, i in ((g1_ref, 0), (b1_ref, 1), (gbout_ref, 4), (g2_ref, 5), (b2_ref, 6)):
        ref[...] = rows[i : i + 1].reshape(width)
    gbqv_ref[...] = rows[2:4]
    gkeys_ref[...] = rows[8:16]
    for copy in going:
        copy.wait()


def sds(*shape):
    return jax.ShapeDtypeStruct(shape, F32)


def vm(*shape):
    return pltpu.VMEM(shape, F32)


def bv(*shape):
    return pltpu.VMEM(shape, BF)


def dma(*shape):
    return pltpu.SemaphoreType.DMA(shape)


def solution(mesh):
    n_dp, n_ex = mesh.shape["dp"], mesh.shape["expert"]

    def on_device(patches, image_ids, pad_mask, ln1_gain, ln1_bias, w_qkv, bias_qv, w_out, bias_out, ln2_gain, ln2_bias,
                  slot_keys, w_in, bias_in, w_down, bias_down, cotangent):
        _, length, width = patches.shape
        owned, _, hidden = w_in.shape
        experts = owned * n_ex
        wide = hidden // LANES
        share = 16
        pair = 2 * HEAD_DIM
        rounds = powers(n_dp) + powers(n_ex) + HALVINGS
        args = dict(zip(INPUTS, (patches, ln1_gain, ln1_bias, w_qkv, bias_qv, image_ids, w_out, bias_out, ln2_gain, ln2_bias,
                                 slot_keys.T, pad_mask, cotangent, w_in, bias_in, w_down, bias_down)))
        names = [n + "_in" for n in INPUTS]
        outs = {"act_out": sds(1, length, width), "gx_out": sds(1, length, width)}
        scratch = {n: pltpu.VMEM(a.shape, a.dtype) for n, a in args.items()}
        scratch.update(
            joined=vm(3 * width, length), context=vm(width, length), attn=vm(HEADS, length, length), block=vm(length, length),
            high=bv(HEADS, length, length), low=bv(HEADS, length, length), kk=bv(HEADS, pair, length),
            qq=bv(HEADS, pair, length), vt=bv(HEADS, pair, length),
            djoined=vm(3 * width, length), normed=vm(width + 8, length), smalls=vm(16, width),
            stats=vm(experts, 8, LANES), near=vm(n_ex - 1, owned, 8, LANES), mine=vm(owned, 8, LANES),
            far=vm(n_dp, owned, 8, LANES), got=vm(owned, 8, LANES), shared=vm(experts, 8, LANES),
            loads=dma(len(args)), sems=dma(2, 6, max(n_dp, n_ex)))
        widths = (width, width, 2 * pair, 2 * pair, pair, pair)
        for c, (kind, cols) in enumerate(zip(PLAN["kinds"], widths)):
            outs[f"c{c}_1"] = sds(width, cols)
            if kind == "halving":
                pieces = [vm(width >> (i + 1), cols) for i in range(HALVINGS)]
                pieces += [vm(rounds - 2 * HALVINGS, width >> HALVINGS, cols), dma(rounds), dma(rounds)]
            else:
                pieces = [vm(width // 2, cols), vm(3, width // 8, cols), vm(n_dp // 2, width // 8, cols), dma(2, 10 + n_dp // 2)]
            scratch[f"c{c}_0"] = vm(width, cols)
            scratch.update({f"c{c}_{2 + i}": piece for i, piece in enumerate(pieces)})
        scratch.update(c6_0=vm(n_ex, share, LANES), c6_1=vm(n_ex - 1, share, LANES), c6_2=vm(n_dp, share, LANES),
                       c6_3=vm(2, share, LANES))
        outs.update(c6_4=sds(n_ex, share, LANES), own=sds(owned, 8, LANES), inner=sds(owned, 2 * wide, LANES))
        names += list(outs) + list(scratch)
        results = pl.pallas_call(
            functools.partial(layer_kernel, n_dp, n_ex, tuple(names)),
            out_shape=list(outs.values()),
            in_specs=[ANY] * len(args),
            out_specs=[VMEM] * len(outs),
            scratch_shapes=list(scratch.values()),
            compiler_params=pltpu.CompilerParams(collective_id=0, has_side_effects=True, vmem_limit_bytes=LAYER_VMEM),
            name="layer",
        )(*args.values())
        act, gx, *grads, small, own, inner = results
        operands = (own, inner, small, act, gx, *grads)
        act, gx, g1, b1, gwqkv, gbqv, gwout, gbout, g2, b2, gkeys, gwin, gbin, gwdown, gbdown = pl.pallas_call(
            finish_kernel,
            out_shape=(sds(1, length, width), sds(1, length, width), sds(width), sds(width), sds(*w_qkv.shape),
                       sds(*bias_qv.shape), sds(*w_out.shape), sds(width), sds(width), sds(width), sds(experts, width),
                       sds(*w_in.shape), sds(*bias_in.shape), sds(*w_down.shape), sds(*bias_down.shape)),
            in_specs=[ANY] * len(operands),
            out_specs=[ANY, ANY, VMEM, VMEM, ANY, VMEM, ANY, VMEM, VMEM, VMEM, VMEM, ANY, VMEM, ANY, VMEM],
            scratch_shapes=[vm(*w_in.shape), vm(*w_down.shape), vm(2, width, pair), *(vm(*a.shape) for a in operands),
                            dma(len(operands)), dma(10 + 6 * owned)],
            compiler_params=pltpu.CompilerParams(vmem_limit_bytes=FINISH_VMEM),
            name="finish",
        )(*operands)
        return (act, gx, g1, b1, gwqkv, gbqv, gwout, gbout, g2, b2, gkeys.T, gwin, gbin, gwdown, gbdown)

    rows = P(("dp", "expert"), None, None)
    flags = P(("dp", "expert"), None)
    e3, e2 = P("expert", None, None), P("expert", None)
    return jax.shard_map(
        on_device,
        mesh=mesh,
        in_specs=(rows, flags, flags) + (P(),) * 9 + (e3, e2, e3, e2, rows),
        out_specs=(rows, rows) + (P(),) * 9 + (e3, e2, e3, e2),
        check_vma=False,
    )
```

time: 231 us -> 84.8 us (0.37)
  waiting for transfers between devices: 93.3 us -> 0 us
  blocking collectives: 40.2 us -> 0 us
  Pallas kernels: 51.5 us -> 83.8 us
  local copies, waits for them, and re-layouts: 31 us -> 0 us
  between operations: 14.2 us -> 0.84 us
    psum x1 -> x0, waiting for transfers between devices: 93.3 us -> none  [on_device(): gwqkv, gwout, small = lax.psum((gwqkv, gwout, small), ('dp', 'expert'))]
    psum x1 -> x0, blocking collectives: 40.2 us -> none  [on_device(): gwqkv, gwout, small = lax.psum((gwqkv, gwout, small), ('dp', 'expert'))]
    pallas_call x3 -> x2, Pallas kernels: 51.5 us -> 83.8 us  [the longest x1 77.1 us: on_device(): pl.pallas_call(functools.partial(layer_kernel, n_dp, n_ex, tuple(names)),...]
    unnamed x59 -> x0, local copies, waits for them, and re-layouts: 25.7 us -> none
    reshape x5 -> x0, local copies, waits for them, and re-layouts: 3.45 us -> none  [on_device(): row = lambda v: v.reshape(1, -1)]
  transfers between devices with their start and end apart: 1 -> 0, of which waited for: 1 -> 0; matrix products, arithmetic and copies ran while one was open for 1% -> 0% of each run, Pallas kernels for 0% -> 0%
where the time goes in v2:
time: 84.8 us; the launch traced here: 84.6 us
  Pallas kernels  83.8 us (99%)
    pallas_call x1, Pallas kernels, on_device(): pl.pallas_call(functools.partial(layer_kernel, n_dp, n_ex, tuple(names)),...  77.1 us
    pallas_call x1, Pallas kernels, on_device(): pl.pallas_call(finish_kernel, out_shape=(sds(1, length, width), sds(1, le...  6.73 us

profile of v2, /device:TPU:0, one launch (start us, length us, event | category | flops | bytes accessed | tf_op | source)
XLA Modules:
  0.0 84.6 jit_solution(13925784137628953754)
XLA Ops:
  0.7 77.1 %layer.1 = (f32[1,512,384]{2,1,0:T(8,128)}, f32[1,512,384]{2,1,0:T(8,128)}, f32[384,384]{1,0:T(8,128)}, f32[384,384]{1,0:T(8,128)}, f32[384,256]{1,0:T(8,128)}, ...) custom-call(f32[1,512,384]{2,1,0:T(8,128)} %refs_0_.1, ...), custom_call_target="tpu_custom_call" | custom-call | tf_op jit(solution)/shard_map/layer/pallas_call | solution.py:644
  77.7 6.7 %finish.1 = (f32[1,512,384]{2,1,0:T(8,128)}, f32[1,512,384]{2,1,0:T(8,128)}, f32[384]{0:T(512)}, f32[384]{0:T(512)}, f32[384,1152]{1,0:T(8,128)}, /*index=5*/f32...) custom-call(f32[2,8,128]{2,1,0:T(8,128)} %get-tuple-element.41.refs_, ...), custom_call_target="tpu_custom_call" | custom-call | tf_op jit(solution)/shard_map/finish/pallas_call | solution.py:655

commit v3 on v2

--- a/solution.py
+++ b/solution.py
@@ -46,10 +46,6 @@
     return center * scale, scale
 
 
-def column(row):
-    return jnp.broadcast_to(row, (8, row.shape[1])).T[:, :1]
-
-
 def load(sources, targets, sems):
     copies = [pltpu.make_async_copy(src, dst, sems.at[i]) for i, (src, dst) in enumerate(zip(sources, targets))]
     for copy in copies:
@@ -153,7 +149,7 @@
     stats_ref, near, mine, far, got, shared_ref, own_ref, inner_ref = (
         at[n] for n in ("stats", "near", "mine", "far", "got", "shared", "own", "inner"))
     win, wdown, bin_ref, bdown_ref = at["win"], at["wdown"], at["bin"], at["bdown"]
-    joined_ref, context_ref, attn_ref, block_ref = at["joined"], at["context"], at["attn"], at["block"]
+    joined_ref, context_ref, attn_ref, share_ref = at["joined"], at["context"], at["attn"], at["share"]
     high_ref, low_ref, kk_ref, qq_ref, vt_ref = at["high"], at["low"], at["kk"], at["qq"], at["vt"]
     djoined_ref, normed_ref, smalls = at["djoined"], at["normed"], at["smalls"]
     sems = at["sems"]
@@ -168,6 +164,7 @@
     ready("x", "g1", "b1")
     x = at["x"][0]
     length, width = x.shape
+    pair = 2 * HEAD_DIM
     half = length // 2
     halves = [slice(half * b, half * (b + 1)) for b in range(2)]
     hat, _ = norm_stats(x)
@@ -180,29 +177,35 @@
     joined_ref[0:width] = (joined[:width] + bias) * scale
     joined_ref[width : 2 * width] = joined[width : 2 * width]
     joined_ref[2 * width :] = joined[2 * width :] + bias_v
-    ids = at["ids"][...].astype(F32)
-    block_ref[...] = jnp.where(column(ids) == ids, 0.0, NEGATIVE)
+    place = lax.broadcasted_iota(jnp.int32, (16, length), 0)
+    same = place == at["ids"][...]
+    pick = jnp.where(same, 1.0, 0.0).astype(BF)
+    bar = jnp.where(same, 0.0, NEGATIVE).astype(BF)
+    ones = jnp.ones((16, length), BF)
     for h in range(HEADS):
         lo = HEAD_DIM * h
         q_hi, q_lo = parts(joined_ref[lo : lo + HEAD_DIM])
         k_hi, k_lo = parts(joined_ref[width + lo : width + lo + HEAD_DIM])
         v_hi, v_lo = parts(joined_ref[2 * width + lo : 2 * width + lo + HEAD_DIM])
-        queries = jnp.concatenate([q_hi, q_hi, q_lo], 0)
-        keys = jnp.concatenate([k_hi, k_lo, k_hi], 0).T
-        values = jnp.concatenate([v_hi, v_lo], 0)
+        queries = jnp.concatenate([q_hi, q_hi, q_lo, pick], 0)
+        keys = jnp.concatenate([k_hi, k_lo, k_hi, bar], 0).T
+        values = jnp.concatenate([v_hi, v_lo, ones], 0)
+        values_low = jnp.concatenate([v_hi, ones], 0)
         kk_ref[h] = jnp.concatenate([k_hi, k_lo], 0)
         qq_ref[h] = jnp.concatenate([q_hi, q_lo], 0)
-        vt_ref[h] = values
+        vt_ref[h] = values[:pair]
         for part in halves:
-            scores = dot(keys, queries[:, part], 1, 0, None) + block_ref[:, part]
+            scores = dot(keys, queries[:, part], 1, 0, None)
             expo = jnp.exp(scores - jnp.max(scores, 0, keepdims=True))
-            attn = expo * (1.0 / jnp.sum(expo, 0, keepdims=True))
-            attn_ref[h, :, part] = attn
-            p_hi, p_lo = parts(attn)
+            attn_ref[h, :, part] = expo
+            p_hi, p_lo = parts(expo)
             high_ref[h, :, part] = p_hi
             low_ref[h, :, part] = p_lo
             both = dot(values, p_hi, 1, 0, None)
-            context_ref[lo : lo + HEAD_DIM, part] = both[:HEAD_DIM] + both[HEAD_DIM:] + dot(v_hi, p_lo, 1, 0, None)
+            rest = dot(values_low, p_lo, 1, 0, None)
+            share = 1.0 / (both[pair : pair + 1] + rest[HEAD_DIM : HEAD_DIM + 1])
+            share_ref[h : h + 1, part] = share
+            context_ref[lo : lo + HEAD_DIM, part] = (both[:HEAD_DIM] + both[HEAD_DIM:pair] + rest[:HEAD_DIM]) * share
     ready("wout", "bout", "g2", "b2", "keys", "live", "cot")
     context = context_ref[...]
     resid = x + dot(context, at["wout"][...], 0, 0) + as_row(at["bout"])
@@ -439,8 +442,13 @@
     outs = []
     for h in range(HEADS):
         lo = HEAD_DIM * h
-        o_hi, o_lo = parts(d_context[lo : lo + HEAD_DIM])
-        outs.append((o_hi, o_lo))
+        scaled = d_context[lo : lo + HEAD_DIM] * share_ref[h : h + 1]
+        o_hi, o_lo = parts(scaled)
+        rowsum = jnp.sum(scaled * context_ref[lo : lo + HEAD_DIM], 0, keepdims=True)
+        r_hi = rowsum.astype(BF).astype(F32)
+        r_mid = (rowsum - r_hi).astype(BF).astype(F32)
+        r_all = jnp.where(place == 0, r_hi, jnp.where(place == 1, r_mid, jnp.where(place == 2, rowsum - r_hi - r_mid, 0.0)))
+        outs.append(jnp.concatenate([o_hi, o_hi, o_lo, r_all.astype(BF)], 0))
         both = jnp.concatenate([o_hi, o_lo], 0)
         d_v = None
         for part in halves:
@@ -453,19 +461,17 @@
     chunks[1][0][...] = grad[:width]
     begin(1)
     smalls[3:4] = grad[width : width + 1]
+    minus = jnp.where(place < 3, -1.0, 0.0).astype(BF)
     launch_at = {1: (2, 0, 2), 3: (3, 2, 4), 4: (4, 4, 5), 5: (5, 5, 6)}
     for h in range(HEADS):
         lo = HEAD_DIM * h
         span = slice(lo, lo + HEAD_DIM)
-        o_hi, o_lo = outs[h]
-        rowsum = jnp.sum(d_context[span] * context_ref[span], 0, keepdims=True)
+        d_out = outs[h]
         v_both, keys, queries = vt_ref[h], kk_ref[h], qq_ref[h]
-        values = jnp.concatenate([v_both, v_both[:HEAD_DIM]], 0).T
-        d_out = jnp.concatenate([o_hi, o_hi, o_lo], 0)
+        values = jnp.concatenate([v_both, v_both[:HEAD_DIM], minus], 0).T
         d_k = None
         for part in halves:
-            d_attn = dot(values, d_out[:, part], 1, 0, None)
-            s_hi, s_lo = parts(attn_ref[h, :, part] * (d_attn - rowsum[:, part]))
+            s_hi, s_lo = parts(attn_ref[h, :, part] * dot(values, d_out[:, part], 1, 0, None))
             both = dot(keys, s_hi, 1, 0, None)
             d_q = both[:HEAD_DIM] + both[HEAD_DIM:] + dot(keys[:HEAD_DIM], s_lo, 1, 0, None)
             djoined_ref[span, part] = d_q * scale
@@ -620,7 +626,7 @@
         outs = {"act_out": sds(1, length, width), "gx_out": sds(1, length, width)}
         scratch = {n: pltpu.VMEM(a.shape, a.dtype) for n, a in args.items()}
         scratch.update(
-            joined=vm(3 * width, length), context=vm(width, length), attn=vm(HEADS, length, length), block=vm(length, length),
+            joined=vm(3 * width, length), context=vm(width, length), attn=vm(HEADS, length, length), share=vm(8, length),
             high=bv(HEADS, length, length), low=bv(HEADS, length, length), kk=bv(HEADS, pair, length),
             qq=bv(HEADS, pair, length), vt=bv(HEADS, pair, length),
             djoined=vm(3 * width, length), normed=vm(width + 8, length), smalls=vm(16, width),

time: 84.8 us -> 79.7 us (0.940)
  Pallas kernels: 83.8 us -> 78.4 us
    pallas_call x1, Pallas kernels: 77.1 us -> 71.7 us  [on_device(): pl.pallas_call(functools.partial(layer_kernel, n_dp, n_ex, tuple(names)),...]
where the time goes in v3:
time: 79.7 us; the launch traced here: 79.2 us
  Pallas kernels  78.4 us (98%)
  between operations  0.82 us (1%)
    pallas_call x1, Pallas kernels, on_device(): pl.pallas_call(functools.partial(layer_kernel, n_dp, n_ex, tuple(names)),...  71.7 us
    pallas_call x1, Pallas kernels, on_device(): pl.pallas_call(finish_kernel, out_shape=(sds(1, length, width), sds(1, le...  6.73 us

profile of v3, /device:TPU:0, one launch (start us, length us, event | category | flops | bytes accessed | tf_op | source)
XLA Modules:
  0.0 79.2 jit_solution(650181916940380009)
XLA Ops:
  0.7 71.7 %layer.1 = (f32[1,512,384]{2,1,0:T(8,128)}, f32[1,512,384]{2,1,0:T(8,128)}, f32[384,384]{1,0:T(8,128)}, f32[384,384]{1,0:T(8,128)}, f32[384,256]{1,0:T(8,128)}, ...) custom-call(f32[1,512,384]{2,1,0:T(8,128)} %refs_0_.1, ...), custom_call_target="tpu_custom_call" | custom-call | tf_op jit(solution)/shard_map/layer/pallas_call | solution.py:650
  72.3 6.7 %finish.1 = (f32[1,512,384]{2,1,0:T(8,128)}, f32[1,512,384]{2,1,0:T(8,128)}, f32[384]{0:T(512)}, f32[384]{0:T(512)}, f32[384,1152]{1,0:T(8,128)}, /*index=5*/f32...) custom-call(f32[2,8,128]{2,1,0:T(8,128)} %get-tuple-element.41.refs_, ...), custom_call_target="tpu_custom_call" | custom-call | tf_op jit(solution)/shard_map/finish/pallas_call | solution.py:661
